TPU v7x, 256 devices: a whole 4x4x8 slice. The times are simulated.
256 devices in a mesh: loop: 32 (over z, x_hi, core), grp: 8 (over y, x_lo).
Axes of the slice: x: 4 (x_hi: 2, x_lo: 2; x = x_hi * 2 + x_lo), y: 4, z: 8, core: 2. Of those that a mesh axis runs over, the one named last changes fastest.
Arguments:
- node_feats: bfloat16 [512, 65536], P(None, ('loop', 'grp')), may hold values from -6 to 6
- tile_vals: bfloat16 [32, 32, 10, 128, 128], P('loop'), may hold values from -0.375 to 0.375
- tile_rows: int32 [32, 32, 10], P('loop'), may hold values from 0 to 15
- tile_cols: int32 [32, 32, 10], P('loop'), may hold values from 0 to 15
- tile_count: int32 [32, 32], P('loop'), may hold values from 0 to 10, as said below
- degree: int32 [65536], P('loop'), may hold values from 1 to 8
- w_self: bfloat16 [512, 512], replicated, may hold values from -0.25 to 0.25
- w_neigh: bfloat16 [512, 512], replicated, may hold values from -0.25 to 0.25
Outputs:
- node_out: bfloat16 [512, 65536], P(None, ('loop', 'grp'))
Inputs may be any that keep to these rules, and one draw needn't show every extreme that they name: Only the first tile_count[j, t] slots of a pair are tiles of the graph; later slots hold values that belong to no edge. Some pair uses all 10 slots in every draw.
All inputs are finite; a program needn't handle non-finite values.
Results may differ from a plain program's by a relative error of at most 0.0035.
Values may be sent and summed in bfloat16 or wider, within the bound.
No kernel may reach another device: no remote copies, remote signals or barrier semaphores. Data moves between devices by JAX's collectives and lax.ppermute only.
A program may use at most 64 MiB of HBM per device.

v0:
```python
import functools

import jax
import jax.numpy as jnp
from jax import lax
from jax.experimental import pallas as pl
from jax.experimental.pallas import tpu as pltpu
from jax.sharding import Mesh
from jax.sharding import PartitionSpec as P


RINGS = 8
SIDES = 2
CORES = 2
REACH = RINGS // 2
BLOCKS = 16
NEAR = 10
VMEM = 3 * 1024 * 1024
RESIDENT = pl.BlockSpec(memory_space=pltpu.VMEM)
SCALARS = pl.BlockSpec(memory_space=pltpu.SMEM)


def cores_at(distance):
    return 1 if distance in (0, REACH) else CORES


def small_call(body, operands, outs):
    return pl.pallas_call(
        body,
        in_specs=[RESIDENT] * len(operands),
        out_specs=[RESIDENT] * len(outs),
        out_shape=outs,
        compiler_params=pltpu.CompilerParams(vmem_limit_bytes=VMEM),
        cost_estimate=pl.CostEstimate(flops=500_000_000, bytes_accessed=1_000_000, transcendentals=0),
    )(*operands)


def target_of(distance, core_turn, side_turn, given):
    mine = lax.axis_index("core")
    by = jnp.where(mine == given, distance, RINGS - distance)
    ring = lax.rem(lax.axis_index("ring") + by, RINGS)
    side = lax.axis_index("side") ^ side_turn
    core = mine ^ given ^ core_turn
    return (ring * SIDES + side) * CORES + core


def add_tiles(total, target, codes, columns, tiles):
    slots, edge = tiles.shape[:2]
    blocks = total.shape[0]
    shift = blocks.bit_length() - 1
    per = columns.shape[2] // edge
    for slot in range(slots):
        code = codes[slot, target]
        row, col = code >> shift, code & (blocks - 1)
        lanes = pl.ds(pl.multiple_of((col & (per - 1)) * edge, edge), edge)
        chosen = columns[col >> (per.bit_length() - 1), :, lanes]
        chosen = jnp.where(row < blocks, chosen, jnp.zeros_like(chosen))
        total[row & (blocks - 1)] += lax.dot_general(
            chosen, tiles[slot], (((1,), (1,)), ((), ())), preferred_element_type=jnp.float32
        )


def copies_of(plan, source, out, done):
    copies = []
    for distance, given in plan:
        for core in range(cores_at(distance)):
            for side in range(SIDES):
                place = len(copies)
                target = target_of(distance, core, side, given)
                copies.append(pltpu.make_async_copy(source.at[target], out.at[place], done.at[place]))
    return copies


def places_of(plan):
    return sum(cores_at(distance) * SIDES for distance, _ in plan)


def tile_kernel(keep, give, first, ahead, codes, columns, tiles, *rest):
    copies = []
    if ahead:
        source, *rest, done = rest
        *rest, out, total = rest
        copies = copies_of(ahead, source, out, done)
    else:
        *rest, total = rest
    for copy in copies:
        copy.start()

    def add(distance, core, side, given):
        target = target_of(distance, core, side, given)
        place = target if first is None else first + core * SIDES + side
        add_tiles(total, target, codes, columns, tiles.at[place])

    if keep is not None:
        partner, late, near, cross = rest[:4]
        rest = rest[4:]

        @pl.loop(0, cores_at(keep))
        def _(core):
            for side in range(SIDES):
                index = core * SIDES + side
                total[...] = partner[index].astype(jnp.float32)
                add(keep, core, side, 0)
                late[index] = total[NEAR:].astype(late.dtype)
                out = near if side == 0 else cross
                out[core] = total[:NEAR].astype(out.dtype)

    if give is not None:
        given = rest[0]

        @pl.loop(0, cores_at(give))
        def _(core):
            for side in range(SIDES):
                total[...] = jnp.zeros_like(total)
                add(give, core, side, 1)
                given[core * SIDES + side] = total[...].astype(given.dtype)

    for copy in copies:
        copy.wait()


def tile_sums(keep, give, first, codes, columns, tiles, partner=None, ahead=(), source=None):
    edge = tiles.shape[2]
    groups, channels, width = columns.shape
    blocks = groups * width // edge
    outs = []
    work = 0
    if keep is not None:
        cores = cores_at(keep)
        work += cores * SIDES
        late = jnp.bfloat16 if keep == REACH else jnp.float32
        outs += [
            jax.ShapeDtypeStruct((cores * SIDES, blocks - NEAR, channels, edge), late),
            jax.ShapeDtypeStruct((cores, NEAR, channels, edge), jnp.float32),
            jax.ShapeDtypeStruct((cores, NEAR, channels, edge), jnp.bfloat16),
        ]
    if give is not None:
        cores = cores_at(give)
        work += cores * SIDES
        outs.append(jax.ShapeDtypeStruct((cores * SIDES, blocks, channels, edge), jnp.bfloat16))
    operands, specs = [columns, tiles], [RESIDENT, RESIDENT]
    scratch = [pltpu.VMEM((blocks, channels, edge), jnp.float32)]
    if ahead:
        operands.append(pltpu.with_memory_space_constraint(source, pltpu.HBM))
        specs.append(pl.BlockSpec(memory_space=pltpu.HBM))
        outs.append(jax.ShapeDtypeStruct((places_of(ahead), *source.shape[1:]), source.dtype))
        scratch.append(pltpu.SemaphoreType.DMA((places_of(ahead),)))
    if partner is not None:
        operands.append(partner)
        specs.append(RESIDENT)
    return pl.pallas_call(
        functools.partial(tile_kernel, keep, give, first, ahead),
        in_specs=[SCALARS] + specs,
        out_specs=[RESIDENT] * len(outs),
        out_shape=outs,
        scratch_shapes=scratch,
        compiler_params=pltpu.CompilerParams(vmem_limit_bytes=VMEM),
        cost_estimate=pl.CostEstimate(
            flops=work * 500_000_000, bytes_accessed=work * 800_000, transcendentals=0
        ),
    )(codes, *operands)


def load_kernel(plan, source, out, done):
    copies = copies_of(plan, source, out, done)
    for copy in copies:
        copy.start()
    for copy in copies:
        copy.wait()


def load(plan, tiles):
    count = places_of(plan)
    return pl.pallas_call(
        functools.partial(load_kernel, plan),
        in_specs=[pl.BlockSpec(memory_space=pltpu.HBM)],
        out_specs=RESIDENT,
        out_shape=jax.ShapeDtypeStruct((count, *tiles.shape[1:]), tiles.dtype),
        scratch_shapes=[pltpu.SemaphoreType.DMA((count,))],
        compiler_params=pltpu.CompilerParams(vmem_limit_bytes=256 * 1024),
        cost_estimate=pl.CostEstimate(flops=2_000_000_000, bytes_accessed=5_000_000, transcendentals=0),
    )(pltpu.with_memory_space_constraint(tiles, pltpu.HBM))


def sum_kernel(has_late, has_near, arrived_late, arrived_near, *refs):
    refs = list(refs)
    arrived = refs.pop(0) if arrived_late or arrived_near else None
    here = refs.pop(0) if has_late else None
    near, crossed = (refs.pop(0), refs.pop(0)) if has_near else (None, None)
    send = refs.pop(0)
    place = 0
    if has_late:
        count, depth = here.shape[:2]
        for index in range(count):
            total = here[index]
            if index < arrived_late:
                total = total + arrived[pl.ds(index * depth, depth)].astype(jnp.float32)
            send[pl.ds(place, depth)] = total.astype(send.dtype)
            place += depth
    if has_near:
        count, depth = near.shape[:2]
        start = arrived_late * (near_gap(near))
        for index in range(count):
            total = near[index] + crossed[index].astype(jnp.float32)
            if index < arrived_near:
                total = total + arrived[pl.ds(start + index * depth, depth)].astype(jnp.float32)
            send[pl.ds(place, depth)] = total.astype(send.dtype)
            place += depth
    if refs:
        depth = near_gap(near)
        moved = refs[0]
        moved[...] = arrived[pl.ds(moved.shape[0], moved.shape[0])]


def near_gap(near):
    return BLOCKS - near.shape[1]


def sums(here, near, crossed, arrived, arrived_late, arrived_near, moved=False):
    operands, blocks = [], 0
    if arrived is not None:
        operands.append(arrived)
    if here is not None:
        operands.append(here)
        blocks += here.shape[0] * here.shape[1]
    if near is not None:
        operands += [near, crossed]
        blocks += near.shape[0] * near.shape[1]
    tail = operands[-1].shape[2:]
    outs = [jax.ShapeDtypeStruct((blocks, *tail), jnp.bfloat16)]
    if moved:
        outs.append(jax.ShapeDtypeStruct((SIDES * near_gap(near), *tail), jnp.bfloat16))
    body = functools.partial(sum_kernel, here is not None, near is not None, arrived_late, arrived_near)
    return small_call(body, operands, outs)


def half_kernel(arrived, out):
    out[...] = arrived[pl.ds(out.shape[0], out.shape[0])]


def second_half(arrived):
    out = jax.ShapeDtypeStruct((arrived.shape[0] // 2, *arrived.shape[1:]), arrived.dtype)
    return small_call(half_kernel, (arrived,), [out])[0]


def across_kernel(here, arrived, moved, send):
    depth = here.shape[1]
    part = pl.ds(depth, depth)
    total = here[1] + arrived[part].astype(jnp.float32) + moved[part].astype(jnp.float32)
    send[...] = total.astype(send.dtype)


def across(here, arrived, moved):
    out = jax.ShapeDtypeStruct(here.shape[1:], jnp.bfloat16)
    return small_call(across_kernel, (here, arrived, moved), [out])[0]


def divide_kernel(near, near_cross, near_same, near_moved, late, late_cross, late_same, late_moved, degree, out):
    for block in range(degree.shape[0]):
        here, cross, same, moved, place = near, near_cross.at[0], near_same, near_moved, block
        if block >= NEAR:
            here, cross, same, moved, place = late, late_cross, late_same, late_moved, block - NEAR
        total = here[0, place] + cross[place].astype(jnp.float32)
        total = total + same[place].astype(jnp.float32) + moved[place].astype(jnp.float32)
        total = total / degree[block : block + 1].astype(jnp.float32)
        out[block // out.shape[1], block % out.shape[1]] = total.astype(out.dtype)


def divide(groups, operands):
    degree = operands[-1]
    blocks, edge = degree.shape
    out = jax.ShapeDtypeStruct((groups, blocks // groups, operands[0].shape[2], edge), jnp.bfloat16)
    return small_call(divide_kernel, operands, [out])[0]


def finish_kernel(base, weight, neighbors, out):
    edge = neighbors.shape[3]
    for part in range(neighbors.shape[1]):
        lanes = slice(part * edge, (part + 1) * edge)
        combined = base[:, lanes] + lax.dot_general(
            weight[...],
            neighbors[:, part].reshape(-1, edge),
            (((0,), (0,)), ((), ())),
            preferred_element_type=jnp.float32,
        )
        hidden = jnp.maximum(combined, 0.0)
        mean_square = jnp.mean(hidden * hidden, axis=0, keepdims=True)
        out[:, lanes] = (hidden * lax.rsqrt(mean_square + 1e-05)).astype(out.dtype)


def finish(base, weight, neighbors):
    return pl.pallas_call(
        finish_kernel,
        out_shape=jax.ShapeDtypeStruct(base.shape, jnp.bfloat16),
        compiler_params=pltpu.CompilerParams(vmem_limit_bytes=10 * 1024 * 1024),
    )(base, weight, neighbors)


def hop(values):
    pairs = []
    for ring in range(RINGS):
        for core in range(CORES):
            pairs.append((ring * CORES + core, (ring + 1 - 2 * core) % RINGS * CORES + core))
    return lax.ppermute(values, ("ring", "core"), pairs)


def swap(values, axis):
    return lax.ppermute(values, axis, [(0, 1), (1, 0)])


def shards(node_feats, tile_vals, tile_rows, tile_cols, tile_count, degree, w_self, w_neigh):
    groups = lax.axis_size("grp")
    features, width = node_feats.shape
    columns = lax.all_to_all(node_feats.reshape(groups, features // groups, width), "grp", split_axis=0, concat_axis=0)
    tiles = tile_vals[0]
    targets, slots, edge = tiles.shape[:3]
    blocks = groups * width // edge
    assert blocks == BLOCKS and (width // edge) & (width // edge - 1) == 0
    active = lax.broadcasted_iota(jnp.int32, (slots, targets), 0) < tile_count
    codes = jnp.where(active, tile_rows[0].T, blocks) * blocks + tile_cols[0].T
    head = load(((REACH, 1), (REACH - 1, 1), (REACH, 0)), tiles)

    def work(keep, give, partner=None, first=None, held=tiles, ahead=()):
        return tile_sums(keep, give, first, codes, columns, held, partner, ahead, tiles)

    (given,) = work(None, REACH, None, 0, head)
    partner = swap(given, "core")
    given, next_tiles = work(None, REACH - 1, None, SIDES, head, ((REACH - 1, 0),))
    late, near, cross = work(REACH, None, partner, SIDES + CORES * SIDES, head)
    message = late.reshape(-1, *late.shape[2:])
    partner = swap(given, "core")
    arrived = hop(message)
    crossed = swap(cross, "side")
    before = near
    late, near, cross = work(3, None, partner, 0, next_tiles)
    (given,) = work(None, 2)
    (message,) = sums(late, before, crossed, arrived, SIDES, 0)
    arrived_near = 1
    for step in (2, 3):
        distance = REACH - step
        partner = swap(given, "core")
        crossed = swap(cross, "side")
        arrived = hop(message)
        before = near
        late, near, cross, given = work(distance, distance - 1, partner)
        (message,) = sums(late, before, crossed, arrived, CORES * SIDES, arrived_near)
        arrived_near = CORES
    partner = swap(given, "core")
    crossed = swap(cross, "side")
    arrived = hop(message)
    before = near
    late, near, cross = work(0, None, partner)
    crossed_last = swap(cross, "side")
    message, moved = sums(None, before, crossed, arrived, CORES * SIDES, CORES, True)
    near_arrived = hop(message)
    moved = swap(moved, "core")
    late_cross = swap(across(late, arrived, moved), "side")
    near_moved = swap(second_half(near_arrived), "core")
    shares = degree.reshape(blocks, edge)
    operands = (near, crossed_last, near_arrived, near_moved, late, late_cross, arrived, moved, shares)
    neighbor = divide(groups, operands)
    gathered = lax.all_to_all(neighbor, "grp", split_axis=0, concat_axis=0)
    base = lax.dot_general(
        w_self, node_feats, (((0,), (0,)), ((), ())), preferred_element_type=jnp.float32
    )
    return finish(base, w_neigh, gathered)


def solution(mesh):
    fine = Mesh(
        mesh.devices.reshape(RINGS, SIDES, CORES, mesh.shape["grp"]), ("ring", "side", "core", "grp")
    )
    loop = ("ring", "side", "core")
    return jax.shard_map(
        shards,
        mesh=fine,
        in_specs=(
            P(None, (*loop, "grp")),
            P(loop, None, None, None, None),
            P(loop, None, None),
            P(loop, None, None),
            P(loop, None),
            P(loop),
            P(),
            P(),
        ),
        out_specs=P(None, (*loop, "grp")),
        check_vma=False,
    )
```

profile of v0, /device:TPU:2, one launch (start us, length us, event | category | flops | bytes accessed | tf_op | source)
XLA Modules:
  0.0 107.3 jit_solution(6603839778915635789)
XLA Ops:
  0.0 6.1 %all-to-all-start = ((bf16[8,64,256]{2,1,0:T(8,128)(2,1)}), bf16[8,64,256]{2,1,0:T(8,128)(2,1)S(1)}, u32[]{:S(2)}, u32[]{:S(2)}) async-start(bf16[8,64,256]{2,1,0:T(8,128)(2,1)} %bitcast.29), calls=%async_computation | async-start | bytes 524288 | tf_op jit(solution)/shard_map/all_to_all | solution.py:314
  6.8 5.4 %all-to-all-done.columns = bf16[8,64,256]{2,1,0:T(8,128)(2,1)S(1)} async-done(((bf16[8,64,256]{2,1,0:T(8,128)(2,1)}), bf16[8,64,256]{2,1,0:T(8,128)(2,1)S(1)}, u32[]{:S(2)}, u32[]{:S(2)}) %all-to-all-start) | async-done | bytes 262176 | tf_op jit(solution)/shard_map/all_to_all | solution.py:314
  12.2 4.0 %copy-done.1 = bf16[1,32,10,128,128]{4,3,2,1,0:T(8,128)(2,1)S(1)} copy-done((bf16[1,32,10,128,128]{4,3,2,1,0:T(8,128)(2,1)S(1)}, bf16[1,32,10,128,128]{4,3,2,1,0:T(8,128)(2,1)}, u32[]{:S(2)}) %copy-start.1) | copy-done | bytes 10485784
  16.2 1.9 %shard_map.82 = bf16[4,16,64,128]{3,2,1,0:T(8,128)(2,1)S(1)} custom-call(s32[10,32]{1,0:T(8,128)S(1)} %bitcast_add_fusion.codes, bf16[8,64,256]{2,1,0:T(8,128)(2,1)S(1)} %all-to-all-done.columns, bf16[32,10,128,128]{3,2,1,0:T(8,128)(2,1)S(1)} %bitcast.21), custom_call_target="tpu_custom_call" | custom-call | flops 2000000000 | bytes 3200000 | tf_op jit(solution)/shard_map/pallas_call | solution.py:151
  18.2 1.9 %shard_map.86.tiles = bf16[8,10,128,128]{3,2,1,0:T(8,128)(2,1)S(1)} custom-call(bf16[32,10,128,128]{3,2,1,0:T(8,128)(2,1)} %bitcast.19), custom_call_target="tpu_custom_call" | custom-call | flops 2000000000 | bytes 5000000 | tf_op jit(solution)/shard_map/pallas_call | solution.py:174
  20.2 2.8 %shard_map.89 = (bf16[4,16,64,128]{3,2,1,0:T(8,128)(2,1)S(1)}, bf16[4,10,128,128]{3,2,1,0:T(8,128)(2,1)S(1)}) custom-call(s32[10,32]{1,0:T(8,128)S(1)} %bitcast_add_fusion.codes, bf16[8,64,256]{2,1,0:T(8,128)(2,1)S(1)} %all-to-all-done.columns, bf16[8,10,128,128]{3,2,1,0:T(8,128)(2,1)S(1)} %shard_map.86.tiles, bf16[32,10,128,128]{3,2,1,0:T(8,128)(2,1)} %bitcast.20), custom_call_target="tpu_custom_call" | custom-call | flops 2000000000 | bytes 3200000 | tf_op jit(solution)/shard_map/pallas_call | solution.py:151
  24.9 1.9 %collective-permute-done.4.rest_0_ = bf16[2,16,64,128]{3,2,1,0:T(8,128)(2,1)S(1)} collective-permute-done((bf16[2,16,64,128]{3,2,1,0:T(8,128)(2,1)S(1)}, bf16[2,16,64,128]{3,2,1,0:T(8,128)(2,1)S(1)}, u32[]{:S(2)}, u32[]{:S(2)}) %collective-permute-start.4) | collective-permute-done | bytes 524320 | tf_op jit(solution)/shard_map/ppermute | solution.py:308
  28.0 2.0 %collective-permute-start.5 = (bf16[12,64,128]{2,1,0:T(8,128)(2,1)S(1)}, bf16[12,64,128]{2,1,0:T(8,128)(2,1)S(1)}, u32[]{:S(2)}, u32[]{:S(2)}) collective-permute-start(bf16[12,64,128]{2,1,0:T(8,128)(2,1)S(1)} %bitcast.28), channel_id=1, source_target_pairs={{0,32},{8,232},{32,64},{40,8},{64,96},{72,40},{96,128},{104,72},{1... | collective-permute-start | bytes 589832 | tf_op jit(solution)/shard_map/ppermute | solution.py:304
  30.0 2.1 %collective-permute-start.7 = (bf16[1,10,64,128]{3,2,1,0:T(8,128)(2,1)S(1)}, bf16[1,10,64,128]{3,2,1,0:T(8,128)(2,1)S(1)}, u32[]{:S(2)}, u32[]{:S(2)}) collective-permute-start(bf16[1,10,64,128]{3,2,1,0:T(8,128)(2,1)S(1)} %get-tuple-element.35), channel_id=1, source_target_pairs={{0,16},{16,0},{1,17},{17,1},{2,18},{18,2},{3,19},{19,3},{4,20},{20... | collective-permute-start | bytes 491528 | tf_op jit(solution)/shard_map/ppermute | solution.py:308
  32.2 3.2 %shard_map.83 = (f32[4,6,64,128]{3,2,1,0:T(8,128)S(1)}, f32[2,10,64,128]{3,2,1,0:T(8,128)S(1)}, bf16[2,10,64,128]{3,2,1,0:T(8,128)(2,1)S(1)}, bf16[4,16,64,128]{3,2,1,0:T(8,128)(2,1)S(1)}) custom-call(s32[10,32]{1,0:T(8,128)S(1)} %bitcast_add_fusion.codes, bf16[8,64,256]{2,1,0:T(8,128)(2,1)S(1)} %all-to-all-done.columns, ...), custom_call_target="tpu_custom_call" | custom-call | flops 4000000000 | bytes 6400000 | tf_op jit(solution)/shard_map/pallas_call | solution.py:151
  35.4 3.6 %collective-permute-start.1 = (bf16[4,16,64,128]{3,2,1,0:T(8,128)(2,1)S(1)}, bf16[4,16,64,128]{3,2,1,0:T(8,128)(2,1)S(1)}, u32[]{:S(2)}, u32[]{:S(2)}) collective-permute-start(bf16[4,16,64,128]{3,2,1,0:T(8,128)(2,1)S(1)} %get-tuple-element.26), channel_id=1, source_target_pairs={{0,8},{8,0},{1,9},{9,1},{2,10},{10,2},{3,11},{11,3},{4,12},{12,4},... | collective-permute-start | bytes 3145736 | tf_op jit(solution)/shard_map/ppermute | solution.py:308
  39.0 1.9 %shard_map.90 = (f32[4,6,64,128]{3,2,1,0:T(8,128)S(1)}, f32[2,10,64,128]{3,2,1,0:T(8,128)S(1)}, bf16[2,10,64,128]{3,2,1,0:T(8,128)(2,1)S(1)}) custom-call(s32[10,32]{1,0:T(8,128)S(1)} %bitcast_add_fusion.codes, bf16[8,64,256]{2,1,0:T(8,128)(2,1)S(1)} %all-to-all-done.columns, bf16[4,10,128,128]{3,2,1,0:T(8,128)(2,1)S(1)} %get-tuple-element.31.tiles, ...), custom_call_target="tpu_custom_call" | custom-call | flops 2000000000 | bytes 3200000 | tf_op jit(solution)/shard_map/pallas_call | solution.py:151
  41.1 1.5 %collective-permute-start.9 = (bf16[2,10,64,128]{3,2,1,0:T(8,128)(2,1)S(1)}, bf16[2,10,64,128]{3,2,1,0:T(8,128)(2,1)S(1)}, u32[]{:S(2)}, u32[]{:S(2)}) collective-permute-start(bf16[2,10,64,128]{3,2,1,0:T(8,128)(2,1)S(1)} %get-tuple-element.38), channel_id=1, source_target_pairs={{0,16},{16,0},{1,17},{17,1},{2,18},{18,2},{3,19},{19,3},{4,20},{20... | collective-permute-start | bytes 983048 | tf_op jit(solution)/shard_map/ppermute | solution.py:308
  42.6 10.6 %collective-permute-done.9.refs_3_ = bf16[2,10,64,128]{3,2,1,0:T(8,128)(2,1)S(1)} collective-permute-done((bf16[2,10,64,128]{3,2,1,0:T(8,128)(2,1)S(1)}, bf16[2,10,64,128]{3,2,1,0:T(8,128)(2,1)S(1)}, u32[]{:S(2)}, u32[]{:S(2)}) %collective-permute-start.9) | collective-permute-done | bytes 327712 | tf_op jit(solution)/shard_map/ppermute | solution.py:308
  53.5 1.5 %collective-permute-start.11 = (bf16[2,10,64,128]{3,2,1,0:T(8,128)(2,1)S(1)}, bf16[2,10,64,128]{3,2,1,0:T(8,128)(2,1)S(1)}, u32[]{:S(2)}, u32[]{:S(2)}) collective-permute-start(bf16[2,10,64,128]{3,2,1,0:T(8,128)(2,1)S(1)} %get-tuple-element.41), channel_id=1, source_target_pairs={{0,16},{16,0},{1,17},{17,1},{2,18},{18,2},{3,19},{19,3},{4,20},{20... | collective-permute-start | bytes 983048 | tf_op jit(solution)/shard_map/ppermute | solution.py:308
  55.0 2.6 %shard_map.84 = (f32[4,6,64,128]{3,2,1,0:T(8,128)S(1)}, f32[2,10,64,128]{3,2,1,0:T(8,128)S(1)}, bf16[2,10,64,128]{3,2,1,0:T(8,128)(2,1)S(1)}, bf16[2,16,64,128]{3,2,1,0:T(8,128)(2,1)S(1)}) custom-call(s32[10,32]{1,0:T(8,128)S(1)} %bitcast_add_fusion.codes, bf16[8,64,256]{2,1,0:T(8,128)(2,1)S(1)} %all-to-all-done.columns, ...), custom_call_target="tpu_custom_call" | custom-call | flops 3000000000 | bytes 4800000 | tf_op jit(solution)/shard_map/pallas_call | solution.py:151
  57.5 7.3 %collective-permute-done.11.refs_3_ = bf16[2,10,64,128]{3,2,1,0:T(8,128)(2,1)S(1)} collective-permute-done((bf16[2,10,64,128]{3,2,1,0:T(8,128)(2,1)S(1)}, bf16[2,10,64,128]{3,2,1,0:T(8,128)(2,1)S(1)}, u32[]{:S(2)}, u32[]{:S(2)}) %collective-permute-start.11) | collective-permute-done | bytes 327712 | tf_op jit(solution)/shard_map/ppermute | solution.py:308
  67.1 9.3 %collective-permute-done.13.refs_2_ = bf16[2,10,64,128]{3,2,1,0:T(8,128)(2,1)S(1)} collective-permute-done((bf16[2,10,64,128]{3,2,1,0:T(8,128)(2,1)S(1)}, bf16[2,10,64,128]{3,2,1,0:T(8,128)(2,1)S(1)}, u32[]{:S(2)}, u32[]{:S(2)}) %collective-permute-start.13) | collective-permute-done | bytes 327712 | tf_op jit(solution)/shard_map/ppermute | solution.py:308
  76.4 2.3 %collective-permute-done.12.refs_0_.arrived.late_same = bf16[44,64,128]{2,1,0:T(8,128)(2,1)S(1)} collective-permute-done((bf16[44,64,128]{2,1,0:T(8,128)(2,1)S(1)}, bf16[44,64,128]{2,1,0:T(8,128)(2,1)S(1)}, u32[]{:S(2)}, u32[]{:S(2)}) %collective-permute-start.12) | collective-permute-done | bytes 720928 | tf_op jit(solution)/shard_map/ppermute | solution.py:304
  79.0 1.3 %shard_map.85 = (f32[2,6,64,128]{3,2,1,0:T(8,128)S(1)}, f32[1,10,64,128]{3,2,1,0:T(8,128)S(1)}, bf16[1,10,64,128]{3,2,1,0:T(8,128)(2,1)S(1)}) custom-call(s32[10,32]{1,0:T(8,128)S(1)} %bitcast_add_fusion.codes, bf16[8,64,256]{2,1,0:T(8,128)(2,1)S(1)} %all-to-all-done.columns, bf16[32,10,128,128]{3,2,1,0:T(8,128)(2,1)S(1)} %bitcast.26, ...), custom_call_target="tpu_custom_call" | custom-call | flops 1000000000 | bytes 1600000 | tf_op jit(solution)/shard_map/pallas_call | solution.py:151
  81.1 6.1 %collective-permute-done.14.arrived.near_same = bf16[20,64,128]{2,1,0:T(8,128)(2,1)S(1)} collective-permute-done((bf16[20,64,128]{2,1,0:T(8,128)(2,1)S(1)}, bf16[20,64,128]{2,1,0:T(8,128)(2,1)S(1)}, u32[]{:S(2)}, u32[]{:S(2)}) %collective-permute-start.14) | collective-permute-done | bytes 327712 | tf_op jit(solution)/shard_map/ppermute | solution.py:304
  88.5 5.6 %collective-permute-done.17.late_cross = bf16[6,64,128]{2,1,0:T(8,128)(2,1)S(1)} collective-permute-done((bf16[6,64,128]{2,1,0:T(8,128)(2,1)S(1)}, bf16[6,64,128]{2,1,0:T(8,128)(2,1)S(1)}, u32[]{:S(2)}, u32[]{:S(2)}) %collective-permute-start.17) | collective-permute-done | bytes 98336 | tf_op jit(solution)/shard_map/ppermute | solution.py:308
  95.0 4.8 %all-to-all-start.1 = ((bf16[8,2,64,128]{3,2,1,0:T(8,128)(2,1)}), bf16[8,2,64,128]{3,2,1,0:T(8,128)(2,1)S(1)}, u32[]{:S(2)}, u32[]{:S(2)}) async-start(bf16[8,2,64,128]{3,2,1,0:T(8,128)(2,1)} %shard_map.97), calls=%async_computation.1 | async-start | bytes 524288 | tf_op jit(solution)/shard_map/all_to_all | solution.py:362
  100.2 5.9 %all-to-all-done.1.neighbors = bf16[8,2,64,128]{3,2,1,0:T(8,128)(2,1)S(1)} async-done(((bf16[8,2,64,128]{3,2,1,0:T(8,128)(2,1)}), bf16[8,2,64,128]{3,2,1,0:T(8,128)(2,1)S(1)}, u32[]{:S(2)}, u32[]{:S(2)}) %all-to-all-start.1) | async-done | bytes 262176 | tf_op jit(solution)/shard_map/all_to_all | solution.py:362
  (52 shorter events, 11.5 us)
Async XLA Ops:
  0.0 99.8 %copy-start = (bf16[512,512]{1,0:T(8,128)(2,1)S(1)}, bf16[512,512]{1,0:T(8,128)(2,1)}, u32[]{:S(2)}) copy-start(bf16[512,512]{1,0:T(8,128)(2,1)} %param.14) | copy-start | bytes 1572868
  0.0 12.2 %all-to-all-start = ((bf16[8,64,256]{2,1,0:T(8,128)(2,1)}), bf16[8,64,256]{2,1,0:T(8,128)(2,1)S(1)}, u32[]{:S(2)}, u32[]{:S(2)}) async-start(bf16[8,64,256]{2,1,0:T(8,128)(2,1)} %bitcast.29), calls=%async_computation | async-start | bytes 524288 | tf_op jit(solution)/shard_map/all_to_all | solution.py:314
  18.1 14.0 %collective-permute-start = (bf16[4,16,64,128]{3,2,1,0:T(8,128)(2,1)S(1)}, bf16[4,16,64,128]{3,2,1,0:T(8,128)(2,1)S(1)}, u32[]{:S(2)}, u32[]{:S(2)}) collective-permute-start(bf16[4,16,64,128]{3,2,1,0:T(8,128)(2,1)S(1)} %shard_map.82), channel_id=1, source_target_pairs={{0,8},{8,0},{1,9},{9,1},{2,10},{10,2},{3,11},{11,3},{4,12},{12,4},... | collective-permute-start | bytes 3145736 | tf_op jit(solution)/shard_map/ppermute | solution.py:308
  18.2 13.9 %slice-start = ((s8[10485760]{0:T(1024)(128)(4,1)}), s8[4194304]{0:T(1024)(128)(4,1)S(1)}, s32[]{:S(2)}) async-start(s8[10485760]{0:T(1024)(128)(4,1)} %bitcast.22), calls=%async_computation.2 | async-start | bytes 8388608
  18.2 13.9 %slice-start.1 = ((s8[10485760]{0:T(1024)(128)(4,1)}), s8[4194304]{0:T(1024)(128)(4,1)S(1)}, s32[]{:S(2)}) async-start(s8[10485760]{0:T(1024)(128)(4,1)} %bitcast.22), calls=%async_computation.3 | async-start | bytes 8388608
  22.9 16.1 %collective-permute-start.6 = (bf16[4,16,64,128]{3,2,1,0:T(8,128)(2,1)S(1)}, bf16[4,16,64,128]{3,2,1,0:T(8,128)(2,1)S(1)}, u32[]{:S(2)}, u32[]{:S(2)}) collective-permute-start(bf16[4,16,64,128]{3,2,1,0:T(8,128)(2,1)S(1)} %get-tuple-element.32), channel_id=1, source_target_pairs={{0,8},{8,0},{1,9},{9,1},{2,10},{10,2},{3,11},{11,3},{4,12},{12,4},... | collective-permute-start | bytes 3145736 | tf_op jit(solution)/shard_map/ppermute | solution.py:308
  24.8 2.0 %collective-permute-start.4 = (bf16[2,16,64,128]{3,2,1,0:T(8,128)(2,1)S(1)}, bf16[2,16,64,128]{3,2,1,0:T(8,128)(2,1)S(1)}, u32[]{:S(2)}, u32[]{:S(2)}) collective-permute-start(bf16[2,16,64,128]{3,2,1,0:T(8,128)(2,1)S(1)} %shard_map.87), channel_id=1, source_target_pairs={{0,8},{8,0},{1,9},{9,1},{2,10},{10,2},{3,11},{11,3},{4,12},{12,4},... | collective-permute-start | bytes 1572872 | tf_op jit(solution)/shard_map/ppermute | solution.py:308
  28.0 12.9 %collective-permute-start.5 = (bf16[12,64,128]{2,1,0:T(8,128)(2,1)S(1)}, bf16[12,64,128]{2,1,0:T(8,128)(2,1)S(1)}, u32[]{:S(2)}, u32[]{:S(2)}) collective-permute-start(bf16[12,64,128]{2,1,0:T(8,128)(2,1)S(1)} %bitcast.28), channel_id=1, source_target_pairs={{0,32},{8,232},{32,64},{40,8},{64,96},{72,40},{96,128},{104,72},{1... | collective-permute-start | bytes 589832 | tf_op jit(solution)/shard_map/ppermute | solution.py:304
  30.0 10.9 %collective-permute-start.7 = (bf16[1,10,64,128]{3,2,1,0:T(8,128)(2,1)S(1)}, bf16[1,10,64,128]{3,2,1,0:T(8,128)(2,1)S(1)}, u32[]{:S(2)}, u32[]{:S(2)}) collective-permute-start(bf16[1,10,64,128]{3,2,1,0:T(8,128)(2,1)S(1)} %get-tuple-element.35), channel_id=1, source_target_pairs={{0,16},{16,0},{1,17},{17,1},{2,18},{18,2},{3,19},{19,3},{4,20},{20... | collective-permute-start | bytes 491528 | tf_op jit(solution)/shard_map/ppermute | solution.py:308
  35.4 19.6 %collective-permute-start.1 = (bf16[4,16,64,128]{3,2,1,0:T(8,128)(2,1)S(1)}, bf16[4,16,64,128]{3,2,1,0:T(8,128)(2,1)S(1)}, u32[]{:S(2)}, u32[]{:S(2)}) collective-permute-start(bf16[4,16,64,128]{3,2,1,0:T(8,128)(2,1)S(1)} %get-tuple-element.26), channel_id=1, source_target_pairs={{0,8},{8,0},{1,9},{9,1},{2,10},{10,2},{3,11},{11,3},{4,12},{12,4},... | collective-permute-start | bytes 3145736 | tf_op jit(solution)/shard_map/ppermute | solution.py:308
  41.0 12.2 %collective-permute-start.8 = (bf16[34,64,128]{2,1,0:T(8,128)(2,1)S(1)}, bf16[34,64,128]{2,1,0:T(8,128)(2,1)S(1)}, u32[]{:S(2)}, u32[]{:S(2)}) collective-permute-start(bf16[34,64,128]{2,1,0:T(8,128)(2,1)S(1)} %shard_map.91), channel_id=1, source_target_pairs={{0,32},{8,232},{32,64},{40,8},{64,96},{72,40},{96,128},{104,72},{1... | collective-permute-start | bytes 1671176 | tf_op jit(solution)/shard_map/ppermute | solution.py:304
  41.1 12.1 %collective-permute-start.9 = (bf16[2,10,64,128]{3,2,1,0:T(8,128)(2,1)S(1)}, bf16[2,10,64,128]{3,2,1,0:T(8,128)(2,1)S(1)}, u32[]{:S(2)}, u32[]{:S(2)}) collective-permute-start(bf16[2,10,64,128]{3,2,1,0:T(8,128)(2,1)S(1)} %get-tuple-element.38), channel_id=1, source_target_pairs={{0,16},{16,0},{1,17},{17,1},{2,18},{18,2},{3,19},{19,3},{4,20},{20... | collective-permute-start | bytes 983048 | tf_op jit(solution)/shard_map/ppermute | solution.py:308
  53.4 12.6 %collective-permute-start.10 = (bf16[44,64,128]{2,1,0:T(8,128)(2,1)S(1)}, bf16[44,64,128]{2,1,0:T(8,128)(2,1)S(1)}, u32[]{:S(2)}, u32[]{:S(2)}) collective-permute-start(bf16[44,64,128]{2,1,0:T(8,128)(2,1)S(1)} %shard_map.92), channel_id=1, source_target_pairs={{0,32},{8,232},{32,64},{40,8},{64,96},{72,40},{96,128},{104,72},{1... | collective-permute-start | bytes 2162696 | tf_op jit(solution)/shard_map/ppermute | solution.py:304
  53.5 11.3 %collective-permute-start.11 = (bf16[2,10,64,128]{3,2,1,0:T(8,128)(2,1)S(1)}, bf16[2,10,64,128]{3,2,1,0:T(8,128)(2,1)S(1)}, u32[]{:S(2)}, u32[]{:S(2)}) collective-permute-start(bf16[2,10,64,128]{3,2,1,0:T(8,128)(2,1)S(1)} %get-tuple-element.41), channel_id=1, source_target_pairs={{0,16},{16,0},{1,17},{17,1},{2,18},{18,2},{3,19},{19,3},{4,20},{20... | collective-permute-start | bytes 983048 | tf_op jit(solution)/shard_map/ppermute | solution.py:308
  66.1 12.6 %collective-permute-start.12 = (bf16[44,64,128]{2,1,0:T(8,128)(2,1)S(1)}, bf16[44,64,128]{2,1,0:T(8,128)(2,1)S(1)}, u32[]{:S(2)}, u32[]{:S(2)}) collective-permute-start(bf16[44,64,128]{2,1,0:T(8,128)(2,1)S(1)} %shard_map.93), channel_id=1, source_target_pairs={{0,32},{8,232},{32,64},{40,8},{64,96},{72,40},{96,128},{104,72},{1... | collective-permute-start | bytes 2162696 | tf_op jit(solution)/shard_map/ppermute | solution.py:304
  66.2 10.2 %collective-permute-start.13 = (bf16[2,10,64,128]{3,2,1,0:T(8,128)(2,1)S(1)}, bf16[2,10,64,128]{3,2,1,0:T(8,128)(2,1)S(1)}, u32[]{:S(2)}, u32[]{:S(2)}) collective-permute-start(bf16[2,10,64,128]{3,2,1,0:T(8,128)(2,1)S(1)} %get-tuple-element.43), channel_id=1, source_target_pairs={{0,16},{16,0},{1,17},{17,1},{2,18},{18,2},{3,19},{19,3},{4,20},{20... | collective-permute-start | bytes 983048 | tf_op jit(solution)/shard_map/ppermute | solution.py:308
  67.1 11.9 %collective-permute-start.2 = (bf16[2,16,64,128]{3,2,1,0:T(8,128)(2,1)S(1)}, bf16[2,16,64,128]{3,2,1,0:T(8,128)(2,1)S(1)}, u32[]{:S(2)}, u32[]{:S(2)}) collective-permute-start(bf16[2,16,64,128]{3,2,1,0:T(8,128)(2,1)S(1)} %get-tuple-element.27), channel_id=1, source_target_pairs={{0,8},{8,0},{1,9},{9,1},{2,10},{10,2},{3,11},{11,3},{4,12},{12,4},... | collective-permute-start | bytes 1572872 | tf_op jit(solution)/shard_map/ppermute | solution.py:308
  78.8 8.4 %collective-permute-start.14 = (bf16[20,64,128]{2,1,0:T(8,128)(2,1)S(1)}, bf16[20,64,128]{2,1,0:T(8,128)(2,1)S(1)}, u32[]{:S(2)}, u32[]{:S(2)}) collective-permute-start(bf16[20,64,128]{2,1,0:T(8,128)(2,1)S(1)} %get-tuple-element.44), channel_id=1, source_target_pairs={{0,32},{8,232},{32,64},{40,8},{64,96},{72,40},{96,128},{104,72},{1... | collective-permute-start | bytes 983048 | tf_op jit(solution)/shard_map/ppermute | solution.py:304
  78.9 8.4 %collective-permute-start.16 = (bf16[12,64,128]{2,1,0:T(8,128)(2,1)S(1)}, bf16[12,64,128]{2,1,0:T(8,128)(2,1)S(1)}, u32[]{:S(2)}, u32[]{:S(2)}) collective-permute-start(bf16[12,64,128]{2,1,0:T(8,128)(2,1)S(1)} %get-tuple-element.46), channel_id=1, source_target_pairs={{0,8},{8,0},{1,9},{9,1},{2,10},{10,2},{3,11},{11,3},{4,12},{12,4},... | collective-permute-start | bytes 589832 | tf_op jit(solution)/shard_map/ppermute | solution.py:308
  80.3 8.2 %collective-permute-start.3 = (bf16[1,10,64,128]{3,2,1,0:T(8,128)(2,1)S(1)}, bf16[1,10,64,128]{3,2,1,0:T(8,128)(2,1)S(1)}, u32[]{:S(2)}, u32[]{:S(2)}) collective-permute-start(bf16[1,10,64,128]{3,2,1,0:T(8,128)(2,1)S(1)} %get-tuple-element.29), channel_id=1, source_target_pairs={{0,16},{16,0},{1,17},{17,1},{2,18},{18,2},{3,19},{19,3},{4,20},{20... | collective-permute-start | bytes 491528 | tf_op jit(solution)/shard_map/ppermute | solution.py:308
  87.2 6.9 %collective-permute-start.15 = (bf16[10,64,128]{2,1,0:T(8,128)(2,1)S(1)}, bf16[10,64,128]{2,1,0:T(8,128)(2,1)S(1)}, u32[]{:S(2)}, u32[]{:S(2)}) collective-permute-start(bf16[10,64,128]{2,1,0:T(8,128)(2,1)S(1)} %shard_map.95), channel_id=1, source_target_pairs={{0,8},{8,0},{1,9},{9,1},{2,10},{10,2},{3,11},{11,3},{4,12},{12,4},... | collective-permute-start | bytes 491528 | tf_op jit(solution)/shard_map/ppermute | solution.py:308
  87.4 18.7 %copy-start.2 = (bf16[512,512]{1,0:T(8,128)(2,1)S(1)}, bf16[512,512]{1,0:T(8,128)(2,1)}, u32[]{:S(2)}) copy-start(bf16[512,512]{1,0:T(8,128)(2,1)} %weight.1) | copy-start | bytes 1572868
  87.4 6.8 %collective-permute-start.17 = (bf16[6,64,128]{2,1,0:T(8,128)(2,1)S(1)}, bf16[6,64,128]{2,1,0:T(8,128)(2,1)S(1)}, u32[]{:S(2)}, u32[]{:S(2)}) collective-permute-start(bf16[6,64,128]{2,1,0:T(8,128)(2,1)S(1)} %shard_map.96), channel_id=1, source_target_pairs={{0,16},{16,0},{1,17},{17,1},{2,18},{18,2},{3,19},{19,3},{4,20},{20... | collective-permute-start | bytes 294920 | tf_op jit(solution)/shard_map/ppermute | solution.py:308
  95.0 11.0 %all-to-all-start.1 = ((bf16[8,2,64,128]{3,2,1,0:T(8,128)(2,1)}), bf16[8,2,64,128]{3,2,1,0:T(8,128)(2,1)S(1)}, u32[]{:S(2)}, u32[]{:S(2)}) async-start(bf16[8,2,64,128]{3,2,1,0:T(8,128)(2,1)} %shard_map.97), calls=%async_computation.1 | async-start | bytes 524288 | tf_op jit(solution)/shard_map/all_to_all | solution.py:362
  (4 other events, 42.5 us)
where the time goes:
time: 108 us; the launch traced here: 107 us
  waiting for transfers between devices  56 us (52%)
  starting transfers between devices  25.2 us (23%)
  Pallas kernels  20.7 us (19%)
  local copies, waits for them, and re-layouts  4.04 us (4%)
    ppermute x13, waiting for transfers between devices, swap(): return lax.ppermute(values, axis, [(0, 1), (1, 0)])  35.2 us
    pallas_call x8, Pallas kernels, tile_sums(): pl.pallas_call(functools.partial(tile_kernel, keep, give, first, ahead),...  16.2 us
    ppermute x13, starting transfers between devices, swap(): return lax.ppermute(values, axis, [(0, 1), (1, 0)])  12 us
    ppermute x5, waiting for transfers between devices, hop(): return lax.ppermute(values, ('ring', 'core'), pairs)  9.54 us
    all_to_all x1, starting transfers between devices, shards(): lax.all_to_all(node_feats.reshape(groups, features // groups, width), 'gr...  6.06 us
    all_to_all x1, waiting for transfers between devices, shards(): gathered = lax.all_to_all(neighbor, 'grp', split_axis=0, concat_axis=0)  5.85 us
    all_to_all x1, waiting for transfers between devices, shards(): lax.all_to_all(node_feats.reshape(groups, features // groups, width), 'gr...  5.41 us
    all_to_all x1, starting transfers between devices, shards(): gathered = lax.all_to_all(neighbor, 'grp', split_axis=0, concat_axis=0)  4.83 us
  transfers between devices with their start and end apart: 20, of which 11 were waited for; matrix products, arithmetic and copies ran while one was open for 1% of the time, Pallas kernels for 15%

commit v1 on v0

--- a/solution.py
+++ b/solution.py
@@ -13,7 +13,6 @@
 SIDES = 2
 CORES = 2
 REACH = RINGS // 2
-BLOCKS = 16
 NEAR = 10
 VMEM = 3 * 1024 * 1024
 RESIDENT = pl.BlockSpec(memory_space=pltpu.VMEM)
@@ -182,56 +181,30 @@
     )(pltpu.with_memory_space_constraint(tiles, pltpu.HBM))
 
 
-def sum_kernel(has_late, has_near, arrived_late, arrived_near, *refs):
-    refs = list(refs)
-    arrived = refs.pop(0) if arrived_late or arrived_near else None
-    here = refs.pop(0) if has_late else None
-    near, crossed = (refs.pop(0), refs.pop(0)) if has_near else (None, None)
-    send = refs.pop(0)
-    place = 0
-    if has_late:
-        count, depth = here.shape[:2]
-        for index in range(count):
-            total = here[index]
-            if index < arrived_late:
-                total = total + arrived[pl.ds(index * depth, depth)].astype(jnp.float32)
-            send[pl.ds(place, depth)] = total.astype(send.dtype)
-            place += depth
-    if has_near:
-        count, depth = near.shape[:2]
-        start = arrived_late * (near_gap(near))
-        for index in range(count):
-            total = near[index] + crossed[index].astype(jnp.float32)
-            if index < arrived_near:
-                total = total + arrived[pl.ds(start + index * depth, depth)].astype(jnp.float32)
-            send[pl.ds(place, depth)] = total.astype(send.dtype)
-            place += depth
-    if refs:
-        depth = near_gap(near)
-        moved = refs[0]
-        moved[...] = arrived[pl.ds(moved.shape[0], moved.shape[0])]
-
-
-def near_gap(near):
-    return BLOCKS - near.shape[1]
-
-
-def sums(here, near, crossed, arrived, arrived_late, arrived_near, moved=False):
-    operands, blocks = [], 0
-    if arrived is not None:
-        operands.append(arrived)
-    if here is not None:
-        operands.append(here)
-        blocks += here.shape[0] * here.shape[1]
-    if near is not None:
-        operands += [near, crossed]
-        blocks += near.shape[0] * near.shape[1]
-    tail = operands[-1].shape[2:]
-    outs = [jax.ShapeDtypeStruct((blocks, *tail), jnp.bfloat16)]
-    if moved:
-        outs.append(jax.ShapeDtypeStruct((SIDES * near_gap(near), *tail), jnp.bfloat16))
-    body = functools.partial(sum_kernel, here is not None, near is not None, arrived_late, arrived_near)
-    return small_call(body, operands, outs)
+def late_kernel(here, arrived, send):
+    for index in range(here.shape[0]):
+        total = here[index]
+        if index < arrived.shape[0]:
+            total = total + arrived[index].astype(jnp.float32)
+        send[index] = total.astype(send.dtype)
+
+
+def pass_late(here, arrived):
+    return small_call(late_kernel, (here, arrived), [jax.ShapeDtypeStruct(here.shape, jnp.bfloat16)])[0]
+
+
+def near_kernel(here, crossed, *rest):
+    *arrived, send = rest
+    for core in range(here.shape[0]):
+        total = here[core] + crossed[core].astype(jnp.float32)
+        if arrived and core < arrived[0].shape[0]:
+            total = total + arrived[0][core].astype(jnp.float32)
+        send[core] = total.astype(send.dtype)
+
+
+def pass_near(here, crossed, *arrived):
+    out = jax.ShapeDtypeStruct(here.shape, jnp.bfloat16)
+    return small_call(near_kernel, (here, crossed, *arrived), [out])[0]
 
 
 def half_kernel(arrived, out):
@@ -244,9 +217,7 @@
 
 
 def across_kernel(here, arrived, moved, send):
-    depth = here.shape[1]
-    part = pl.ds(depth, depth)
-    total = here[1] + arrived[part].astype(jnp.float32) + moved[part].astype(jnp.float32)
+    total = here[1] + arrived[1].astype(jnp.float32) + moved[1].astype(jnp.float32)
     send[...] = total.astype(send.dtype)
 
 
@@ -255,13 +226,13 @@
     return small_call(across_kernel, (here, arrived, moved), [out])[0]
 
 
-def divide_kernel(near, near_cross, near_same, near_moved, late, late_cross, late_same, late_moved, degree, out):
+def divide_kernel(near, near_cross, near_same, near_turned, late, late_cross, late_same, late_turned, degree, out):
     for block in range(degree.shape[0]):
-        here, cross, same, moved, place = near, near_cross.at[0], near_same, near_moved, block
+        here, cross, same, turned, place = near, near_cross.at[0], near_same, near_turned, block
         if block >= NEAR:
-            here, cross, same, moved, place = late, late_cross, late_same, late_moved, block - NEAR
+            here, cross, same, turned, place = late, late_cross, late_same, late_turned, block - NEAR
         total = here[0, place] + cross[place].astype(jnp.float32)
-        total = total + same[place].astype(jnp.float32) + moved[place].astype(jnp.float32)
+        total = total + same[0, place].astype(jnp.float32) + turned[0, place].astype(jnp.float32)
         total = total / degree[block : block + 1].astype(jnp.float32)
         out[block // out.shape[1], block % out.shape[1]] = total.astype(out.dtype)
 
@@ -315,7 +286,7 @@
     tiles = tile_vals[0]
     targets, slots, edge = tiles.shape[:3]
     blocks = groups * width // edge
-    assert blocks == BLOCKS and (width // edge) & (width // edge - 1) == 0
+    assert blocks & (blocks - 1) == 0 and (width // edge) & (width // edge - 1) == 0
     active = lax.broadcasted_iota(jnp.int32, (slots, targets), 0) < tile_count
     codes = jnp.where(active, tile_rows[0].T, blocks) * blocks + tile_cols[0].T
     head = load(((REACH, 1), (REACH - 1, 1), (REACH, 0)), tiles)
@@ -327,37 +298,31 @@
     partner = swap(given, "core")
     given, next_tiles = work(None, REACH - 1, None, SIDES, head, ((REACH - 1, 0),))
     late, near, cross = work(REACH, None, partner, SIDES + CORES * SIDES, head)
-    message = late.reshape(-1, *late.shape[2:])
-    partner = swap(given, "core")
-    arrived = hop(message)
-    crossed = swap(cross, "side")
-    before = near
-    late, near, cross = work(3, None, partner, 0, next_tiles)
-    (given,) = work(None, 2)
-    (message,) = sums(late, before, crossed, arrived, SIDES, 0)
-    arrived_near = 1
-    for step in (2, 3):
+    message, near_back = late, ()
+    for step in range(1, REACH + 1):
         distance = REACH - step
         partner = swap(given, "core")
         crossed = swap(cross, "side")
         arrived = hop(message)
         before = near
-        late, near, cross, given = work(distance, distance - 1, partner)
-        (message,) = sums(late, before, crossed, arrived, CORES * SIDES, arrived_near)
-        arrived_near = CORES
-    partner = swap(given, "core")
+        if step == 1:
+            (given,) = work(None, distance - 1)
+            late, near, cross = work(distance, None, partner, 0, next_tiles)
+        elif distance:
+            late, near, cross, given = work(distance, distance - 1, partner)
+        else:
+            late, near, cross = work(distance, None, partner)
+        if distance:
+            message = pass_late(late, arrived)
+        else:
+            moved = swap(second_half(arrived), "core")
+            late_cross = swap(across(late, arrived, moved), "side")
+        near_message = pass_near(before, crossed, *near_back)
+        near_back = (hop(near_message),)
     crossed = swap(cross, "side")
-    arrived = hop(message)
-    before = near
-    late, near, cross = work(0, None, partner)
-    crossed_last = swap(cross, "side")
-    message, moved = sums(None, before, crossed, arrived, CORES * SIDES, CORES, True)
-    near_arrived = hop(message)
-    moved = swap(moved, "core")
-    late_cross = swap(across(late, arrived, moved), "side")
-    near_moved = swap(second_half(near_arrived), "core")
+    near_moved = swap(second_half(*near_back), "core")
     shares = degree.reshape(blocks, edge)
-    operands = (near, crossed_last, near_arrived, near_moved, late, late_cross, arrived, moved, shares)
+    operands = (near, crossed, *near_back, near_moved, late, late_cross, arrived, moved, shares)
     neighbor = divide(groups, operands)
     gathered = lax.all_to_all(neighbor, "grp", split_axis=0, concat_axis=0)
     base = lax.dot_general(

time: 108 us -> 101 us (0.935)
  waiting for transfers between devices: 56 us -> 43.9 us
  starting transfers between devices: 25.2 us -> 30.7 us
    ppermute x13, waiting for transfers between devices: 35.2 us -> 12.5 us  [swap(): return lax.ppermute(values, axis, [(0, 1), (1, 0)])]
    ppermute x5 -> x8, waiting for transfers between devices: 9.54 us -> 20.1 us  [hop(): return lax.ppermute(values, ('ring', 'core'), pairs)]
    ppermute x5 -> x8, starting transfers between devices: 2.35 us -> 6.39 us  [hop(): return lax.ppermute(values, ('ring', 'core'), pairs)]
    ppermute x13, starting transfers between devices: 12 us -> 13.4 us  [swap(): return lax.ppermute(values, axis, [(0, 1), (1, 0)])]
  transfers between devices with their start and end apart: 20 -> 23, of which waited for: 11 -> 12; matrix products, arithmetic and copies ran while one was open for 1% -> 1% of each run, Pallas kernels for 15% -> 17%
where the time goes in v1:
time: 101 us
  waiting for transfers between devices  43.9 us (43%)
  starting transfers between devices  30.7 us (30%)
  Pallas kernels  20.9 us (21%)
  local copies, waits for them, and re-layouts  4.04 us (4%)
    ppermute x8, waiting for transfers between devices, hop(): return lax.ppermute(values, ('ring', 'core'), pairs)  20.1 us
    pallas_call x8, Pallas kernels, tile_sums(): pl.pallas_call(functools.partial(tile_kernel, keep, give, first, ahead),...  16.3 us
    ppermute x13, starting transfers between devices, swap(): return lax.ppermute(values, axis, [(0, 1), (1, 0)])  13.4 us
    ppermute x13, waiting for transfers between devices, swap(): return lax.ppermute(values, axis, [(0, 1), (1, 0)])  12.5 us
    ppermute x8, starting transfers between devices, hop(): return lax.ppermute(values, ('ring', 'core'), pairs)  6.39 us
    all_to_all x1, starting transfers between devices, shards(): lax.all_to_all(node_feats.reshape(groups, features // groups, width), 'gr...  6.06 us
    all_to_all x1, waiting for transfers between devices, shards(): gathered = lax.all_to_all(neighbor, 'grp', split_axis=0, concat_axis=0)  5.85 us
    all_to_all x1, waiting for transfers between devices, shards(): lax.all_to_all(node_feats.reshape(groups, features // groups, width), 'gr...  5.41 us
  transfers between devices with their start and end apart: 23, of which 12 were waited for; matrix products, arithmetic and copies ran while one was open for 1% of the time, Pallas kernels for 17%

profile of v1, /device:TPU:2, one launch (start us, length us, event | category | flops | bytes accessed | tf_op | source)
XLA Modules:
  0.0 100.8 jit_solution(8015243422569610664)
XLA Ops:
  0.0 6.1 %all-to-all-start = ((bf16[8,64,256]{2,1,0:T(8,128)(2,1)}), bf16[8,64,256]{2,1,0:T(8,128)(2,1)S(1)}, u32[]{:S(2)}, u32[]{:S(2)}) async-start(bf16[8,64,256]{2,1,0:T(8,128)(2,1)} %bitcast.27), calls=%async_computation | async-start | bytes 524288 | tf_op jit(solution)/shard_map/all_to_all | solution.py:285
  6.8 5.4 %all-to-all-done.columns = bf16[8,64,256]{2,1,0:T(8,128)(2,1)S(1)} async-done(((bf16[8,64,256]{2,1,0:T(8,128)(2,1)}), bf16[8,64,256]{2,1,0:T(8,128)(2,1)S(1)}, u32[]{:S(2)}, u32[]{:S(2)}) %all-to-all-start) | async-done | bytes 262176 | tf_op jit(solution)/shard_map/all_to_all | solution.py:285
  12.2 4.0 %copy-done.1 = bf16[1,32,10,128,128]{4,3,2,1,0:T(8,128)(2,1)S(1)} copy-done((bf16[1,32,10,128,128]{4,3,2,1,0:T(8,128)(2,1)S(1)}, bf16[1,32,10,128,128]{4,3,2,1,0:T(8,128)(2,1)}, u32[]{:S(2)}) %copy-start.1) | copy-done | bytes 10485784
  16.2 1.9 %shard_map.82 = bf16[4,16,64,128]{3,2,1,0:T(8,128)(2,1)S(1)} custom-call(s32[10,32]{1,0:T(8,128)S(1)} %bitcast_add_fusion.codes, bf16[8,64,256]{2,1,0:T(8,128)(2,1)S(1)} %all-to-all-done.columns, bf16[32,10,128,128]{3,2,1,0:T(8,128)(2,1)S(1)} %bitcast.20), custom_call_target="tpu_custom_call" | custom-call | flops 2000000000 | bytes 3200000 | tf_op jit(solution)/shard_map/pallas_call | solution.py:150
  18.2 1.9 %shard_map.86.tiles = bf16[8,10,128,128]{3,2,1,0:T(8,128)(2,1)S(1)} custom-call(bf16[32,10,128,128]{3,2,1,0:T(8,128)(2,1)} %bitcast.18), custom_call_target="tpu_custom_call" | custom-call | flops 2000000000 | bytes 5000000 | tf_op jit(solution)/shard_map/pallas_call | solution.py:173
  20.2 2.8 %shard_map.87 = (bf16[4,16,64,128]{3,2,1,0:T(8,128)(2,1)S(1)}, bf16[4,10,128,128]{3,2,1,0:T(8,128)(2,1)S(1)}) custom-call(s32[10,32]{1,0:T(8,128)S(1)} %bitcast_add_fusion.codes, bf16[8,64,256]{2,1,0:T(8,128)(2,1)S(1)} %all-to-all-done.columns, bf16[8,10,128,128]{3,2,1,0:T(8,128)(2,1)S(1)} %shard_map.86.tiles, bf16[32,10,128,128]{3,2,1,0:T(8,128)(2,1)} %bitcast.19), custom_call_target="tpu_custom_call" | custom-call | flops 2000000000 | bytes 3200000 | tf_op jit(solution)/shard_map/pallas_call | solution.py:150
  24.9 3.2 %shard_map.83 = (f32[4,6,64,128]{3,2,1,0:T(8,128)S(1)}, f32[2,10,64,128]{3,2,1,0:T(8,128)S(1)}, bf16[2,10,64,128]{3,2,1,0:T(8,128)(2,1)S(1)}, bf16[4,16,64,128]{3,2,1,0:T(8,128)(2,1)S(1)}) custom-call(s32[10,32]{1,0:T(8,128)S(1)} %bitcast_add_fusion.codes, bf16[8,64,256]{2,1,0:T(8,128)(2,1)S(1)} %all-to-all-done.columns, ...), custom_call_target="tpu_custom_call" | custom-call | flops 4000000000 | bytes 6400000 | tf_op jit(solution)/shard_map/pallas_call | solution.py:150
  30.0 2.2 %collective-permute-start.9 = (bf16[1,10,64,128]{3,2,1,0:T(8,128)(2,1)S(1)}, bf16[1,10,64,128]{3,2,1,0:T(8,128)(2,1)S(1)}, u32[]{:S(2)}, u32[]{:S(2)}) collective-permute-start(bf16[1,10,64,128]{3,2,1,0:T(8,128)(2,1)S(1)} %get-tuple-element.37), channel_id=1, source_target_pairs={{0,16},{16,0},{1,17},{17,1},{2,18},{18,2},{3,19},{19,3},{4,20},{20... | collective-permute-start | bytes 491528 | tf_op jit(solution)/shard_map/ppermute | solution.py:279
  32.2 1.9 %shard_map.88 = (f32[4,6,64,128]{3,2,1,0:T(8,128)S(1)}, f32[2,10,64,128]{3,2,1,0:T(8,128)S(1)}, bf16[2,10,64,128]{3,2,1,0:T(8,128)(2,1)S(1)}) custom-call(s32[10,32]{1,0:T(8,128)S(1)} %bitcast_add_fusion.codes, bf16[8,64,256]{2,1,0:T(8,128)(2,1)S(1)} %all-to-all-done.columns, bf16[4,10,128,128]{3,2,1,0:T(8,128)(2,1)S(1)} %get-tuple-element.32.tiles, ...), custom_call_target="tpu_custom_call" | custom-call | flops 2000000000 | bytes 3200000 | tf_op jit(solution)/shard_map/pallas_call | solution.py:150
  35.6 1.9 %collective-permute-start.15 = (bf16[2,6,64,128]{3,2,1,0:T(8,128)(2,1)S(1)}, bf16[2,6,64,128]{3,2,1,0:T(8,128)(2,1)S(1)}, u32[]{:S(2)}, u32[]{:S(2)}) collective-permute-start(bf16[2,6,64,128]{3,2,1,0:T(8,128)(2,1)S(1)} %get-tuple-element.42), channel_id=1, source_target_pairs={{0,32},{8,232},{32,64},{40,8},{64,96},{72,40},{96,128},{104,72},{1... | collective-permute-start | bytes 589832 | tf_op jit(solution)/shard_map/ppermute | solution.py:275
  37.8 2.0 %collective-permute-start.10 = (bf16[1,10,64,128]{3,2,1,0:T(8,128)(2,1)S(1)}, bf16[1,10,64,128]{3,2,1,0:T(8,128)(2,1)S(1)}, u32[]{:S(2)}, u32[]{:S(2)}) collective-permute-start(bf16[1,10,64,128]{3,2,1,0:T(8,128)(2,1)S(1)} %shard_map.91), channel_id=1, source_target_pairs={{0,32},{8,232},{32,64},{40,8},{64,96},{72,40},{96,128},{104,72},{1... | collective-permute-start | bytes 491528 | tf_op jit(solution)/shard_map/ppermute | solution.py:275
  39.8 5.3 %collective-permute-done.15.arrived = bf16[2,6,64,128]{3,2,1,0:T(8,128)(2,1)S(1)} collective-permute-done((bf16[2,6,64,128]{3,2,1,0:T(8,128)(2,1)S(1)}, bf16[2,6,64,128]{3,2,1,0:T(8,128)(2,1)S(1)}, u32[]{:S(2)}, u32[]{:S(2)}) %collective-permute-start.15) | collective-permute-done | bytes 196640 | tf_op jit(solution)/shard_map/ppermute | solution.py:275
  45.3 2.2 %collective-permute-start.5 = (bf16[2,10,64,128]{3,2,1,0:T(8,128)(2,1)S(1)}, bf16[2,10,64,128]{3,2,1,0:T(8,128)(2,1)S(1)}, u32[]{:S(2)}, u32[]{:S(2)}) collective-permute-start(bf16[2,10,64,128]{3,2,1,0:T(8,128)(2,1)S(1)} %get-tuple-element.31), channel_id=1, source_target_pairs={{0,16},{16,0},{1,17},{17,1},{2,18},{18,2},{3,19},{19,3},{4,20},{20... | collective-permute-start | bytes 983048 | tf_op jit(solution)/shard_map/ppermute | solution.py:279
  47.7 6.6 %collective-permute-done.16.arrived = bf16[4,6,64,128]{3,2,1,0:T(8,128)(2,1)S(1)} collective-permute-done((bf16[4,6,64,128]{3,2,1,0:T(8,128)(2,1)S(1)}, bf16[4,6,64,128]{3,2,1,0:T(8,128)(2,1)S(1)}, u32[]{:S(2)}, u32[]{:S(2)}) %collective-permute-start.16) | collective-permute-done | bytes 393248 | tf_op jit(solution)/shard_map/ppermute | solution.py:275
  54.4 2.6 %collective-permute-done.5.crossed = bf16[2,10,64,128]{3,2,1,0:T(8,128)(2,1)S(1)} collective-permute-done((bf16[2,10,64,128]{3,2,1,0:T(8,128)(2,1)S(1)}, bf16[2,10,64,128]{3,2,1,0:T(8,128)(2,1)S(1)}, u32[]{:S(2)}, u32[]{:S(2)}) %collective-permute-start.5) | collective-permute-done | bytes 327712 | tf_op jit(solution)/shard_map/ppermute | solution.py:279
  58.2 2.6 %shard_map.84 = (f32[4,6,64,128]{3,2,1,0:T(8,128)S(1)}, f32[2,10,64,128]{3,2,1,0:T(8,128)S(1)}, bf16[2,10,64,128]{3,2,1,0:T(8,128)(2,1)S(1)}, bf16[2,16,64,128]{3,2,1,0:T(8,128)(2,1)S(1)}) custom-call(s32[10,32]{1,0:T(8,128)S(1)} %bitcast_add_fusion.codes, bf16[8,64,256]{2,1,0:T(8,128)(2,1)S(1)} %all-to-all-done.columns, ...), custom_call_target="tpu_custom_call" | custom-call | flops 3000000000 | bytes 4800000 | tf_op jit(solution)/shard_map/pallas_call | solution.py:150
  60.8 2.2 %collective-permute-start.4 = (bf16[2,10,64,128]{3,2,1,0:T(8,128)(2,1)S(1)}, bf16[2,10,64,128]{3,2,1,0:T(8,128)(2,1)S(1)}, u32[]{:S(2)}, u32[]{:S(2)}) collective-permute-start(bf16[2,10,64,128]{3,2,1,0:T(8,128)(2,1)S(1)} %get-tuple-element.29), channel_id=1, source_target_pairs={{0,16},{16,0},{1,17},{17,1},{2,18},{18,2},{3,19},{19,3},{4,20},{20... | collective-permute-start | bytes 983048 | tf_op jit(solution)/shard_map/ppermute | solution.py:279
  64.1 2.9 %collective-permute-done.12.rest_0_ = bf16[2,10,64,128]{3,2,1,0:T(8,128)(2,1)S(1)} collective-permute-done((bf16[2,10,64,128]{3,2,1,0:T(8,128)(2,1)S(1)}, bf16[2,10,64,128]{3,2,1,0:T(8,128)(2,1)S(1)}, u32[]{:S(2)}, u32[]{:S(2)}) %collective-permute-start.12) | collective-permute-done | bytes 327712 | tf_op jit(solution)/shard_map/ppermute | solution.py:275
  66.9 5.3 %collective-permute-done.4.crossed = bf16[2,10,64,128]{3,2,1,0:T(8,128)(2,1)S(1)} collective-permute-done((bf16[2,10,64,128]{3,2,1,0:T(8,128)(2,1)S(1)}, bf16[2,10,64,128]{3,2,1,0:T(8,128)(2,1)S(1)}, u32[]{:S(2)}, u32[]{:S(2)}) %collective-permute-start.4) | collective-permute-done | bytes 327712 | tf_op jit(solution)/shard_map/ppermute | solution.py:279
  76.4 4.3 %collective-permute-done.13.arrived.near_same = bf16[2,10,64,128]{3,2,1,0:T(8,128)(2,1)S(1)} collective-permute-done((bf16[2,10,64,128]{3,2,1,0:T(8,128)(2,1)S(1)}, bf16[2,10,64,128]{3,2,1,0:T(8,128)(2,1)S(1)}, u32[]{:S(2)}, u32[]{:S(2)}) %collective-permute-start.13) | collective-permute-done | bytes 327712 | tf_op jit(solution)/shard_map/ppermute | solution.py:275
  80.9 2.4 %collective-permute-start.20 = (bf16[6,64,128]{2,1,0:T(8,128)(2,1)S(1)}, bf16[6,64,128]{2,1,0:T(8,128)(2,1)S(1)}, u32[]{:S(2)}, u32[]{:S(2)}) collective-permute-start(bf16[6,64,128]{2,1,0:T(8,128)(2,1)S(1)} %shard_map.100), channel_id=1, source_target_pairs={{0,16},{16,0},{1,17},{17,1},{2,18},{18,2},{3,19},{19,3},{4,20},{20... | collective-permute-start | bytes 294920 | tf_op jit(solution)/shard_map/ppermute | solution.py:279
  83.3 4.4 %collective-permute-done.20.late_cross = bf16[6,64,128]{2,1,0:T(8,128)(2,1)S(1)} collective-permute-done((bf16[6,64,128]{2,1,0:T(8,128)(2,1)S(1)}, bf16[6,64,128]{2,1,0:T(8,128)(2,1)S(1)}, u32[]{:S(2)}, u32[]{:S(2)}) %collective-permute-start.20) | collective-permute-done | bytes 98336 | tf_op jit(solution)/shard_map/ppermute | solution.py:279
  88.5 4.9 %all-to-all-start.1 = ((bf16[8,2,64,128]{3,2,1,0:T(8,128)(2,1)}), bf16[8,2,64,128]{3,2,1,0:T(8,128)(2,1)S(1)}, u32[]{:S(2)}, u32[]{:S(2)}) async-start(bf16[8,2,64,128]{3,2,1,0:T(8,128)(2,1)} %shard_map.101), calls=%async_computation.1 | async-start | bytes 524288 | tf_op jit(solution)/shard_map/all_to_all | solution.py:327
  93.7 5.8 %all-to-all-done.1.neighbors = bf16[8,2,64,128]{3,2,1,0:T(8,128)(2,1)S(1)} async-done(((bf16[8,2,64,128]{3,2,1,0:T(8,128)(2,1)}), bf16[8,2,64,128]{3,2,1,0:T(8,128)(2,1)S(1)}, u32[]{:S(2)}, u32[]{:S(2)}) %all-to-all-start.1) | async-done | bytes 262176 | tf_op jit(solution)/shard_map/all_to_all | solution.py:327
  (62 shorter events, 15.7 us)
Async XLA Ops:
  0.0 93.4 %copy-start = (bf16[512,512]{1,0:T(8,128)(2,1)S(1)}, bf16[512,512]{1,0:T(8,128)(2,1)}, u32[]{:S(2)}) copy-start(bf16[512,512]{1,0:T(8,128)(2,1)} %param.14) | copy-start | bytes 1572868
  0.0 12.2 %all-to-all-start = ((bf16[8,64,256]{2,1,0:T(8,128)(2,1)}), bf16[8,64,256]{2,1,0:T(8,128)(2,1)S(1)}, u32[]{:S(2)}, u32[]{:S(2)}) async-start(bf16[8,64,256]{2,1,0:T(8,128)(2,1)} %bitcast.27), calls=%async_computation | async-start | bytes 524288 | tf_op jit(solution)/shard_map/all_to_all | solution.py:285
  18.1 6.8 %collective-permute-start = (bf16[4,16,64,128]{3,2,1,0:T(8,128)(2,1)S(1)}, bf16[4,16,64,128]{3,2,1,0:T(8,128)(2,1)S(1)}, u32[]{:S(2)}, u32[]{:S(2)}) collective-permute-start(bf16[4,16,64,128]{3,2,1,0:T(8,128)(2,1)S(1)} %shard_map.82), channel_id=1, source_target_pairs={{0,8},{8,0},{1,9},{9,1},{2,10},{10,2},{3,11},{11,3},{4,12},{12,4},... | collective-permute-start | bytes 3145736 | tf_op jit(solution)/shard_map/ppermute | solution.py:279
  22.9 9.3 %collective-permute-start.6 = (bf16[4,16,64,128]{3,2,1,0:T(8,128)(2,1)S(1)}, bf16[4,16,64,128]{3,2,1,0:T(8,128)(2,1)S(1)}, u32[]{:S(2)}, u32[]{:S(2)}) collective-permute-start(bf16[4,16,64,128]{3,2,1,0:T(8,128)(2,1)S(1)} %get-tuple-element.33), channel_id=1, source_target_pairs={{0,8},{8,0},{1,9},{9,1},{2,10},{10,2},{3,11},{11,3},{4,12},{12,4},... | collective-permute-start | bytes 3145736 | tf_op jit(solution)/shard_map/ppermute | solution.py:279
  24.8 4.0 %collective-permute-start.8 = (bf16[2,16,64,128]{3,2,1,0:T(8,128)(2,1)S(1)}, bf16[2,16,64,128]{3,2,1,0:T(8,128)(2,1)S(1)}, u32[]{:S(2)}, u32[]{:S(2)}) collective-permute-start(bf16[2,16,64,128]{3,2,1,0:T(8,128)(2,1)S(1)} %shard_map.89), channel_id=1, source_target_pairs={{0,8},{8,0},{1,9},{9,1},{2,10},{10,2},{3,11},{11,3},{4,12},{12,4},... | collective-permute-start | bytes 1572872 | tf_op jit(solution)/shard_map/ppermute | solution.py:279
  28.2 30.0 %collective-permute-start.1 = (bf16[4,16,64,128]{3,2,1,0:T(8,128)(2,1)S(1)}, bf16[4,16,64,128]{3,2,1,0:T(8,128)(2,1)S(1)}, u32[]{:S(2)}, u32[]{:S(2)}) collective-permute-start(bf16[4,16,64,128]{3,2,1,0:T(8,128)(2,1)S(1)} %get-tuple-element.24), channel_id=1, source_target_pairs={{0,8},{8,0},{1,9},{9,1},{2,10},{10,2},{3,11},{11,3},{4,12},{12,4},... | collective-permute-start | bytes 3145736 | tf_op jit(solution)/shard_map/ppermute | solution.py:279
  30.0 7.7 %collective-permute-start.9 = (bf16[1,10,64,128]{3,2,1,0:T(8,128)(2,1)S(1)}, bf16[1,10,64,128]{3,2,1,0:T(8,128)(2,1)S(1)}, u32[]{:S(2)}, u32[]{:S(2)}) collective-permute-start(bf16[1,10,64,128]{3,2,1,0:T(8,128)(2,1)S(1)} %get-tuple-element.37), channel_id=1, source_target_pairs={{0,16},{16,0},{1,17},{17,1},{2,18},{18,2},{3,19},{19,3},{4,20},{20... | collective-permute-start | bytes 491528 | tf_op jit(solution)/shard_map/ppermute | solution.py:279
  34.1 13.4 %collective-permute-start.7 = (bf16[2,10,64,128]{3,2,1,0:T(8,128)(2,1)S(1)}, bf16[2,10,64,128]{3,2,1,0:T(8,128)(2,1)S(1)}, u32[]{:S(2)}, u32[]{:S(2)}) collective-permute-start(bf16[2,10,64,128]{3,2,1,0:T(8,128)(2,1)S(1)} %get-tuple-element.35), channel_id=1, source_target_pairs={{0,16},{16,0},{1,17},{17,1},{2,18},{18,2},{3,19},{19,3},{4,20},{20... | collective-permute-start | bytes 983048 | tf_op jit(solution)/shard_map/ppermute | solution.py:279
  35.6 9.5 %collective-permute-start.15 = (bf16[2,6,64,128]{3,2,1,0:T(8,128)(2,1)S(1)}, bf16[2,6,64,128]{3,2,1,0:T(8,128)(2,1)S(1)}, u32[]{:S(2)}, u32[]{:S(2)}) collective-permute-start(bf16[2,6,64,128]{3,2,1,0:T(8,128)(2,1)S(1)} %get-tuple-element.42), channel_id=1, source_target_pairs={{0,32},{8,232},{32,64},{40,8},{64,96},{72,40},{96,128},{104,72},{1... | collective-permute-start | bytes 589832 | tf_op jit(solution)/shard_map/ppermute | solution.py:275
  37.8 9.7 %collective-permute-start.10 = (bf16[1,10,64,128]{3,2,1,0:T(8,128)(2,1)S(1)}, bf16[1,10,64,128]{3,2,1,0:T(8,128)(2,1)S(1)}, u32[]{:S(2)}, u32[]{:S(2)}) collective-permute-start(bf16[1,10,64,128]{3,2,1,0:T(8,128)(2,1)S(1)} %shard_map.91), channel_id=1, source_target_pairs={{0,32},{8,232},{32,64},{40,8},{64,96},{72,40},{96,128},{104,72},{1... | collective-permute-start | bytes 491528 | tf_op jit(solution)/shard_map/ppermute | solution.py:275
  45.2 9.1 %collective-permute-start.16 = (bf16[4,6,64,128]{3,2,1,0:T(8,128)(2,1)S(1)}, bf16[4,6,64,128]{3,2,1,0:T(8,128)(2,1)S(1)}, u32[]{:S(2)}, u32[]{:S(2)}) collective-permute-start(bf16[4,6,64,128]{3,2,1,0:T(8,128)(2,1)S(1)} %shard_map.96), channel_id=1, source_target_pairs={{0,32},{8,232},{32,64},{40,8},{64,96},{72,40},{96,128},{104,72},{1... | collective-permute-start | bytes 1179656 | tf_op jit(solution)/shard_map/ppermute | solution.py:275
  45.3 11.8 %collective-permute-start.5 = (bf16[2,10,64,128]{3,2,1,0:T(8,128)(2,1)S(1)}, bf16[2,10,64,128]{3,2,1,0:T(8,128)(2,1)S(1)}, u32[]{:S(2)}, u32[]{:S(2)}) collective-permute-start(bf16[2,10,64,128]{3,2,1,0:T(8,128)(2,1)S(1)} %get-tuple-element.31), channel_id=1, source_target_pairs={{0,16},{16,0},{1,17},{17,1},{2,18},{18,2},{3,19},{19,3},{4,20},{20... | collective-permute-start | bytes 983048 | tf_op jit(solution)/shard_map/ppermute | solution.py:279
  47.6 10.2 %collective-permute-start.11 = (bf16[2,10,64,128]{3,2,1,0:T(8,128)(2,1)S(1)}, bf16[2,10,64,128]{3,2,1,0:T(8,128)(2,1)S(1)}, u32[]{:S(2)}, u32[]{:S(2)}) collective-permute-start(bf16[2,10,64,128]{3,2,1,0:T(8,128)(2,1)S(1)} %shard_map.92), channel_id=1, source_target_pairs={{0,32},{8,232},{32,64},{40,8},{64,96},{72,40},{96,128},{104,72},{1... | collective-permute-start | bytes 983048 | tf_op jit(solution)/shard_map/ppermute | solution.py:275
  54.4 9.1 %collective-permute-start.17 = (bf16[4,6,64,128]{3,2,1,0:T(8,128)(2,1)S(1)}, bf16[4,6,64,128]{3,2,1,0:T(8,128)(2,1)S(1)}, u32[]{:S(2)}, u32[]{:S(2)}) collective-permute-start(bf16[4,6,64,128]{3,2,1,0:T(8,128)(2,1)S(1)} %shard_map.97), channel_id=1, source_target_pairs={{0,32},{8,232},{32,64},{40,8},{64,96},{72,40},{96,128},{104,72},{1... | collective-permute-start | bytes 1179656 | tf_op jit(solution)/shard_map/ppermute | solution.py:275
  57.9 9.1 %collective-permute-start.12 = (bf16[2,10,64,128]{3,2,1,0:T(8,128)(2,1)S(1)}, bf16[2,10,64,128]{3,2,1,0:T(8,128)(2,1)S(1)}, u32[]{:S(2)}, u32[]{:S(2)}) collective-permute-start(bf16[2,10,64,128]{3,2,1,0:T(8,128)(2,1)S(1)} %shard_map.93), channel_id=1, source_target_pairs={{0,32},{8,232},{32,64},{40,8},{64,96},{72,40},{96,128},{104,72},{1... | collective-permute-start | bytes 983048 | tf_op jit(solution)/shard_map/ppermute | solution.py:275
  60.8 11.5 %collective-permute-start.4 = (bf16[2,10,64,128]{3,2,1,0:T(8,128)(2,1)S(1)}, bf16[2,10,64,128]{3,2,1,0:T(8,128)(2,1)S(1)}, u32[]{:S(2)}, u32[]{:S(2)}) collective-permute-start(bf16[2,10,64,128]{3,2,1,0:T(8,128)(2,1)S(1)} %get-tuple-element.29), channel_id=1, source_target_pairs={{0,16},{16,0},{1,17},{17,1},{2,18},{18,2},{3,19},{19,3},{4,20},{20... | collective-permute-start | bytes 983048 | tf_op jit(solution)/shard_map/ppermute | solution.py:279
  63.0 10.8 %collective-permute-start.2 = (bf16[2,16,64,128]{3,2,1,0:T(8,128)(2,1)S(1)}, bf16[2,16,64,128]{3,2,1,0:T(8,128)(2,1)S(1)}, u32[]{:S(2)}, u32[]{:S(2)}) collective-permute-start(bf16[2,16,64,128]{3,2,1,0:T(8,128)(2,1)S(1)} %get-tuple-element.25), channel_id=1, source_target_pairs={{0,8},{8,0},{1,9},{9,1},{2,10},{10,2},{3,11},{11,3},{4,12},{12,4},... | collective-permute-start | bytes 1572872 | tf_op jit(solution)/shard_map/ppermute | solution.py:279
  63.5 10.2 %collective-permute-start.18 = (bf16[4,6,64,128]{3,2,1,0:T(8,128)(2,1)S(1)}, bf16[4,6,64,128]{3,2,1,0:T(8,128)(2,1)S(1)}, u32[]{:S(2)}, u32[]{:S(2)}) collective-permute-start(bf16[4,6,64,128]{3,2,1,0:T(8,128)(2,1)S(1)} %shard_map.98), channel_id=1, source_target_pairs={{0,32},{8,232},{32,64},{40,8},{64,96},{72,40},{96,128},{104,72},{1... | collective-permute-start | bytes 1179656 | tf_op jit(solution)/shard_map/ppermute | solution.py:275
  72.3 8.4 %collective-permute-start.13 = (bf16[2,10,64,128]{3,2,1,0:T(8,128)(2,1)S(1)}, bf16[2,10,64,128]{3,2,1,0:T(8,128)(2,1)S(1)}, u32[]{:S(2)}, u32[]{:S(2)}) collective-permute-start(bf16[2,10,64,128]{3,2,1,0:T(8,128)(2,1)S(1)} %shard_map.94), channel_id=1, source_target_pairs={{0,32},{8,232},{32,64},{40,8},{64,96},{72,40},{96,128},{104,72},{1... | collective-permute-start | bytes 983048 | tf_op jit(solution)/shard_map/ppermute | solution.py:275
  73.7 7.1 %collective-permute-start.19 = (bf16[2,6,64,128]{3,2,1,0:T(8,128)(2,1)S(1)}, bf16[2,6,64,128]{3,2,1,0:T(8,128)(2,1)S(1)}, u32[]{:S(2)}, u32[]{:S(2)}) collective-permute-start(bf16[2,6,64,128]{3,2,1,0:T(8,128)(2,1)S(1)} %shard_map.99), channel_id=1, source_target_pairs={{0,8},{8,0},{1,9},{9,1},{2,10},{10,2},{3,11},{11,3},{4,12},{12,4},... | collective-permute-start | bytes 589832 | tf_op jit(solution)/shard_map/ppermute | solution.py:279
  75.1 12.5 %collective-permute-start.3 = (bf16[1,10,64,128]{3,2,1,0:T(8,128)(2,1)S(1)}, bf16[1,10,64,128]{3,2,1,0:T(8,128)(2,1)S(1)}, u32[]{:S(2)}, u32[]{:S(2)}) collective-permute-start(bf16[1,10,64,128]{3,2,1,0:T(8,128)(2,1)S(1)} %get-tuple-element.27), channel_id=1, source_target_pairs={{0,16},{16,0},{1,17},{17,1},{2,18},{18,2},{3,19},{19,3},{4,20},{20... | collective-permute-start | bytes 491528 | tf_op jit(solution)/shard_map/ppermute | solution.py:279
  80.7 6.9 %collective-permute-start.14 = (bf16[1,10,64,128]{3,2,1,0:T(8,128)(2,1)S(1)}, bf16[1,10,64,128]{3,2,1,0:T(8,128)(2,1)S(1)}, u32[]{:S(2)}, u32[]{:S(2)}) collective-permute-start(bf16[1,10,64,128]{3,2,1,0:T(8,128)(2,1)S(1)} %shard_map.95), channel_id=1, source_target_pairs={{0,8},{8,0},{1,9},{9,1},{2,10},{10,2},{3,11},{11,3},{4,12},{12,4},... | collective-permute-start | bytes 491528 | tf_op jit(solution)/shard_map/ppermute | solution.py:279
  80.9 6.8 %collective-permute-start.20 = (bf16[6,64,128]{2,1,0:T(8,128)(2,1)S(1)}, bf16[6,64,128]{2,1,0:T(8,128)(2,1)S(1)}, u32[]{:S(2)}, u32[]{:S(2)}) collective-permute-start(bf16[6,64,128]{2,1,0:T(8,128)(2,1)S(1)} %shard_map.100), channel_id=1, source_target_pairs={{0,16},{16,0},{1,17},{17,1},{2,18},{18,2},{3,19},{19,3},{4,20},{20... | collective-permute-start | bytes 294920 | tf_op jit(solution)/shard_map/ppermute | solution.py:279
  88.5 11.1 %all-to-all-start.1 = ((bf16[8,2,64,128]{3,2,1,0:T(8,128)(2,1)}), bf16[8,2,64,128]{3,2,1,0:T(8,128)(2,1)S(1)}, u32[]{:S(2)}, u32[]{:S(2)}) async-start(bf16[8,2,64,128]{3,2,1,0:T(8,128)(2,1)} %shard_map.101), calls=%async_computation.1 | async-start | bytes 524288 | tf_op jit(solution)/shard_map/all_to_all | solution.py:327
  (7 other events, 66.1 us)

commit v2 on v1

--- a/solution.py
+++ b/solution.py
@@ -13,7 +13,7 @@
 SIDES = 2
 CORES = 2
 REACH = RINGS // 2
-NEAR = 10
+NEAR = 9
 VMEM = 3 * 1024 * 1024
 RESIDENT = pl.BlockSpec(memory_space=pltpu.VMEM)
 SCALARS = pl.BlockSpec(memory_space=pltpu.SMEM)
@@ -74,51 +74,54 @@
     return sum(cores_at(distance) * SIDES for distance, _ in plan)
 
 
-def tile_kernel(keep, give, first, ahead, codes, columns, tiles, *rest):
+def tile_kernel(keep, give, first, ahead, offset, codes, columns, tiles, *rest):
     copies = []
     if ahead:
         source, *rest, done = rest
-        *rest, out, total = rest
+        *rest, out, even, odd = rest
         copies = copies_of(ahead, source, out, done)
     else:
-        *rest, total = rest
+        *rest, even, odd = rest
     for copy in copies:
         copy.start()
 
-    def add(distance, core, side, given):
+    def add(total, distance, core, side, given):
         target = target_of(distance, core, side, given)
         place = target if first is None else first + core * SIDES + side
         add_tiles(total, target, codes, columns, tiles.at[place])
 
     if keep is not None:
-        partner, late, near, cross = rest[:4]
-        rest = rest[4:]
-
-        @pl.loop(0, cores_at(keep))
-        def _(core):
+        partner, rest = rest[0], rest[1:]
+        for core in range(cores_at(keep)):
             for side in range(SIDES):
                 index = core * SIDES + side
-                total[...] = partner[index].astype(jnp.float32)
-                add(keep, core, side, 0)
-                late[index] = total[NEAR:].astype(late.dtype)
-                out = near if side == 0 else cross
-                out[core] = total[:NEAR].astype(out.dtype)
-
-    if give is not None:
-        given = rest[0]
-
-        @pl.loop(0, cores_at(give))
-        def _(core):
+                total = odd if side else even
+                total[...] = partner[offset + index].astype(jnp.float32)
+                add(total, keep, core, side, 0)
+                if keep == REACH:
+                    rest[0][index] = total[...].astype(rest[0].dtype)
+                else:
+                    late, near, cross = rest[:3]
+                    late[index] = total[NEAR:].astype(late.dtype)
+                    out = near if side == 0 else cross
+                    out[core] = total[:NEAR].astype(out.dtype)
+        rest = rest[1:] if keep == REACH else rest[3:]
+
+    place = 0
+    for distance in give:
+        for core in range(cores_at(distance)):
             for side in range(SIDES):
+                total = odd if side else even
                 total[...] = jnp.zeros_like(total)
-                add(give, core, side, 1)
-                given[core * SIDES + side] = total[...].astype(given.dtype)
+                add(total, distance, core, side, 1)
+                rest[0][place] = total[...].astype(rest[0].dtype)
+                place += 1
 
     for copy in copies:
         copy.wait()
 
 
-def tile_sums(keep, give, first, codes, columns, tiles, partner=None, ahead=(), source=None):
+def tile_sums(keep, give, first, codes, columns, tiles, partner=None, ahead=(), source=None, offset=0):
     edge = tiles.shape[2]
     groups, channels, width = columns.shape
     blocks = groups * width // edge
@@ -127,18 +130,21 @@
     if keep is not None:
         cores = cores_at(keep)
         work += cores * SIDES
-        late = jnp.bfloat16 if keep == REACH else jnp.float32
-        outs += [
-            jax.ShapeDtypeStruct((cores * SIDES, blocks - NEAR, channels, edge), late),
-            jax.ShapeDtypeStruct((cores, NEAR, channels, edge), jnp.float32),
-            jax.ShapeDtypeStruct((cores, NEAR, channels, edge), jnp.bfloat16),
-        ]
-    if give is not None:
-        cores = cores_at(give)
-        work += cores * SIDES
-        outs.append(jax.ShapeDtypeStruct((cores * SIDES, blocks, channels, edge), jnp.bfloat16))
+        if keep == REACH:
+            outs.append(jax.ShapeDtypeStruct((cores * SIDES, blocks, channels, edge), jnp.bfloat16))
+        else:
+            crossing = jnp.float32 if keep == REACH - 1 else jnp.bfloat16
+            outs += [
+                jax.ShapeDtypeStruct((cores * SIDES, blocks - NEAR, channels, edge), jnp.float32),
+                jax.ShapeDtypeStruct((cores, NEAR, channels, edge), jnp.float32),
+                jax.ShapeDtypeStruct((cores, NEAR, channels, edge), crossing),
+            ]
+    if give:
+        count = sum(cores_at(distance) * SIDES for distance in give)
+        work += count
+        outs.append(jax.ShapeDtypeStruct((count, blocks, channels, edge), jnp.bfloat16))
     operands, specs = [columns, tiles], [RESIDENT, RESIDENT]
-    scratch = [pltpu.VMEM((blocks, channels, edge), jnp.float32)]
+    scratch = [pltpu.VMEM((blocks, channels, edge), jnp.float32)] * 2
     if ahead:
         operands.append(pltpu.with_memory_space_constraint(source, pltpu.HBM))
         specs.append(pl.BlockSpec(memory_space=pltpu.HBM))
@@ -148,7 +154,7 @@
         operands.append(partner)
         specs.append(RESIDENT)
     return pl.pallas_call(
-        functools.partial(tile_kernel, keep, give, first, ahead),
+        functools.partial(tile_kernel, keep, give, first, ahead, offset),
         in_specs=[SCALARS] + specs,
         out_specs=[RESIDENT] * len(outs),
         out_shape=outs,
@@ -179,6 +185,30 @@
         compiler_params=pltpu.CompilerParams(vmem_limit_bytes=256 * 1024),
         cost_estimate=pl.CostEstimate(flops=2_000_000_000, bytes_accessed=5_000_000, transcendentals=0),
     )(pltpu.with_memory_space_constraint(tiles, pltpu.HBM))
+
+
+def first_kernel(late, near, cross, arrived, send, base, crossing):
+    for index in range(late.shape[0]):
+        total = late[index]
+        if index < arrived.shape[0]:
+            total = total + arrived[index, pl.ds(NEAR, total.shape[0])].astype(jnp.float32)
+        send[index] = total.astype(send.dtype)
+    for core in range(near.shape[0]):
+        mine, other = near[core], cross[core]
+        if core == 0:
+            mine = mine + arrived[0, pl.ds(0, NEAR)].astype(jnp.float32)
+            other = other + arrived[1, pl.ds(0, NEAR)].astype(jnp.float32)
+        base[core] = mine
+        crossing[core] = other.astype(crossing.dtype)
+
+
+def pass_first(late, near, cross, arrived):
+    outs = [
+        jax.ShapeDtypeStruct(late.shape, jnp.bfloat16),
+        jax.ShapeDtypeStruct(near.shape, jnp.float32),
+        jax.ShapeDtypeStruct(near.shape, jnp.bfloat16),
+    ]
+    return small_call(first_kernel, (late, near, cross, arrived), outs)
 
 
 def late_kernel(here, arrived, send):
@@ -291,27 +321,27 @@
     codes = jnp.where(active, tile_rows[0].T, blocks) * blocks + tile_cols[0].T
     head = load(((REACH, 1), (REACH - 1, 1), (REACH, 0)), tiles)
 
-    def work(keep, give, partner=None, first=None, held=tiles, ahead=()):
-        return tile_sums(keep, give, first, codes, columns, held, partner, ahead, tiles)
-
-    (given,) = work(None, REACH, None, 0, head)
+    def work(keep, give, partner=None, first=None, held=tiles, ahead=(), offset=0):
+        return tile_sums(keep, give, first, codes, columns, held, partner, ahead, tiles, offset)
+
+    (given,) = work(None, (REACH,), None, 0, head)
     partner = swap(given, "core")
-    given, next_tiles = work(None, REACH - 1, None, SIDES, head, ((REACH - 1, 0),))
-    late, near, cross = work(REACH, None, partner, SIDES + CORES * SIDES, head)
-    message, near_back = late, ()
-    for step in range(1, REACH + 1):
+    given, next_tiles = work(None, (REACH - 1,), None, SIDES, head, ((REACH - 1, 0),))
+    (message,) = work(REACH, (), partner, SIDES + CORES * SIDES, head)
+    partner = swap(given, "core")
+    arrived = hop(message)
+    (given,) = work(None, tuple(range(REACH - 2, -1, -1)))
+    late, near, cross = work(REACH - 1, (), partner, 0, next_tiles)
+    partner = swap(given, "core")
+    message, near, cross = pass_first(late, near, cross, arrived)
+    near_back = ()
+    for step in range(2, REACH + 1):
         distance = REACH - step
-        partner = swap(given, "core")
         crossed = swap(cross, "side")
         arrived = hop(message)
         before = near
-        if step == 1:
-            (given,) = work(None, distance - 1)
-            late, near, cross = work(distance, None, partner, 0, next_tiles)
-        elif distance:
-            late, near, cross, given = work(distance, distance - 1, partner)
-        else:
-            late, near, cross = work(distance, None, partner)
+        offset = (step - 2) * CORES * SIDES
+        late, near, cross = work(distance, (), partner, offset=offset)
         if distance:
             message = pass_late(late, arrived)
         else:

time: 101 us -> 104 us (1.030)
  waiting for transfers between devices: 43.9 us -> 51.9 us
  starting transfers between devices: 30.7 us -> 26.5 us
    ppermute x8 -> x7, waiting for transfers between devices: 20.1 us -> 27.1 us  [hop(): return lax.ppermute(values, ('ring', 'core'), pairs)]
    ppermute x8 -> x7, starting transfers between devices: 6.39 us -> 4.08 us  [hop(): return lax.ppermute(values, ('ring', 'core'), pairs)]
    ppermute x13 -> x10, starting transfers between devices: 13.4 us -> 11.9 us  [swap(): return lax.ppermute(values, axis, [(0, 1), (1, 0)])]
    ppermute x13 -> x10, waiting for transfers between devices: 12.5 us -> 13.5 us  [swap(): return lax.ppermute(values, axis, [(0, 1), (1, 0)])]
  transfers between devices with their start and end apart: 23 -> 19, of which waited for: 12 -> 12; matrix products, arithmetic and copies ran while one was open for 1% -> 1% of each run, Pallas kernels for 17% -> 14%
where the time goes in v2:
time: 104 us
  waiting for transfers between devices  51.9 us (50%)
  starting transfers between devices  26.5 us (25%)
  Pallas kernels  20 us (19%)
  local copies, waits for them, and re-layouts  4.04 us (4%)
    ppermute x7, waiting for transfers between devices, hop(): return lax.ppermute(values, ('ring', 'core'), pairs)  27.1 us
    pallas_call x8, Pallas kernels, tile_sums(): pl.pallas_call(functools.partial(tile_kernel, keep, give, first, ahead, o...  15.6 us
    ppermute x10, waiting for transfers between devices, swap(): return lax.ppermute(values, axis, [(0, 1), (1, 0)])  13.5 us
    ppermute x10, starting transfers between devices, swap(): return lax.ppermute(values, axis, [(0, 1), (1, 0)])  11.9 us
    all_to_all x1, starting transfers between devices, shards(): lax.all_to_all(node_feats.reshape(groups, features // groups, width), 'gr...  6.06 us
    all_to_all x1, waiting for transfers between devices, shards(): gathered = lax.all_to_all(neighbor, 'grp', split_axis=0, concat_axis=0)  5.84 us
    all_to_all x1, waiting for transfers between devices, shards(): lax.all_to_all(node_feats.reshape(groups, features // groups, width), 'gr...  5.41 us
    all_to_all x1, starting transfers between devices, shards(): gathered = lax.all_to_all(neighbor, 'grp', split_axis=0, concat_axis=0)  4.48 us
  transfers between devices with their start and end apart: 19, of which 12 were waited for; matrix products, arithmetic and copies ran while one was open for 1% of the time, Pallas kernels for 14%

profile of v2, /device:TPU:2, one launch (start us, length us, event | category | flops | bytes accessed | tf_op | source)
XLA Modules:
  0.0 103.8 jit_solution(11847737637959327537)
XLA Ops:
  0.0 6.1 %all-to-all-start = ((bf16[8,64,256]{2,1,0:T(8,128)(2,1)}), bf16[8,64,256]{2,1,0:T(8,128)(2,1)S(1)}, u32[]{:S(2)}, u32[]{:S(2)}) async-start(bf16[8,64,256]{2,1,0:T(8,128)(2,1)} %bitcast.27), calls=%async_computation | async-start | bytes 524288 | tf_op jit(solution)/shard_map/all_to_all | solution.py:315
  6.8 5.4 %all-to-all-done.columns = bf16[8,64,256]{2,1,0:T(8,128)(2,1)S(1)} async-done(((bf16[8,64,256]{2,1,0:T(8,128)(2,1)}), bf16[8,64,256]{2,1,0:T(8,128)(2,1)S(1)}, u32[]{:S(2)}, u32[]{:S(2)}) %all-to-all-start) | async-done | bytes 262176 | tf_op jit(solution)/shard_map/all_to_all | solution.py:315
  12.2 4.0 %copy-done.1 = bf16[1,32,10,128,128]{4,3,2,1,0:T(8,128)(2,1)S(1)} copy-done((bf16[1,32,10,128,128]{4,3,2,1,0:T(8,128)(2,1)S(1)}, bf16[1,32,10,128,128]{4,3,2,1,0:T(8,128)(2,1)}, u32[]{:S(2)}) %copy-start.1) | copy-done | bytes 10485784
  16.2 3.0 %shard_map.82 = bf16[10,16,64,128]{3,2,1,0:T(8,128)(2,1)S(1)} custom-call(s32[10,32]{1,0:T(8,128)S(1)} %bitcast_add_fusion.codes, bf16[8,64,256]{2,1,0:T(8,128)(2,1)S(1)} %all-to-all-done.columns, bf16[32,10,128,128]{3,2,1,0:T(8,128)(2,1)S(1)} %bitcast.20), custom_call_target="tpu_custom_call" | custom-call | flops 5000000000 | bytes 8000000 | tf_op jit(solution)/shard_map/pallas_call | solution.py:156
  19.3 1.8 %shard_map.86.tiles = bf16[8,10,128,128]{3,2,1,0:T(8,128)(2,1)S(1)} custom-call(bf16[32,10,128,128]{3,2,1,0:T(8,128)(2,1)} %bitcast.18), custom_call_target="tpu_custom_call" | custom-call | flops 2000000000 | bytes 5000000 | tf_op jit(solution)/shard_map/pallas_call | solution.py:179
  21.0 3.5 %shard_map.87 = (bf16[4,16,64,128]{3,2,1,0:T(8,128)(2,1)S(1)}, bf16[4,10,128,128]{3,2,1,0:T(8,128)(2,1)S(1)}) custom-call(s32[10,32]{1,0:T(8,128)S(1)} %bitcast_add_fusion.codes, bf16[8,64,256]{2,1,0:T(8,128)(2,1)S(1)} %all-to-all-done.columns, bf16[8,10,128,128]{3,2,1,0:T(8,128)(2,1)S(1)} %shard_map.86.tiles, bf16[32,10,128,128]{3,2,1,0:T(8,128)(2,1)} %bitcast.19), custom_call_target="tpu_custom_call" | custom-call | flops 2000000000 | bytes 3200000 | tf_op jit(solution)/shard_map/pallas_call | solution.py:156
  26.6 1.9 %collective-permute-done.5.rest_0_ = bf16[2,16,64,128]{3,2,1,0:T(8,128)(2,1)S(1)} collective-permute-done((bf16[2,16,64,128]{3,2,1,0:T(8,128)(2,1)S(1)}, bf16[2,16,64,128]{3,2,1,0:T(8,128)(2,1)S(1)}, u32[]{:S(2)}, u32[]{:S(2)}) %collective-permute-start.5) | collective-permute-done | bytes 524320 | tf_op jit(solution)/shard_map/ppermute | solution.py:309
  29.7 2.0 %collective-permute-start.6 = (bf16[2,16,64,128]{3,2,1,0:T(8,128)(2,1)S(1)}, bf16[2,16,64,128]{3,2,1,0:T(8,128)(2,1)S(1)}, u32[]{:S(2)}, u32[]{:S(2)}) collective-permute-start(bf16[2,16,64,128]{3,2,1,0:T(8,128)(2,1)S(1)} %shard_map.90), channel_id=1, source_target_pairs={{0,32},{8,232},{32,64},{40,8},{64,96},{72,40},{96,128},{104,72},{1... | collective-permute-start | bytes 1572872 | tf_op jit(solution)/shard_map/ppermute | solution.py:305
  33.4 9.4 %collective-permute-done.6.arrived = bf16[2,16,64,128]{3,2,1,0:T(8,128)(2,1)S(1)} collective-permute-done((bf16[2,16,64,128]{3,2,1,0:T(8,128)(2,1)S(1)}, bf16[2,16,64,128]{3,2,1,0:T(8,128)(2,1)S(1)}, u32[]{:S(2)}, u32[]{:S(2)}) %collective-permute-start.6) | collective-permute-done | bytes 524320 | tf_op jit(solution)/shard_map/ppermute | solution.py:305
  43.0 2.2 %collective-permute-start.7 = (bf16[2,9,64,128]{3,2,1,0:T(8,128)(2,1)S(1)}, bf16[2,9,64,128]{3,2,1,0:T(8,128)(2,1)S(1)}, u32[]{:S(2)}, u32[]{:S(2)}) collective-permute-start(bf16[2,9,64,128]{3,2,1,0:T(8,128)(2,1)S(1)} %get-tuple-element.34), channel_id=1, source_target_pairs={{0,16},{16,0},{1,17},{17,1},{2,18},{18,2},{3,19},{19,3},{4,20},{20... | collective-permute-start | bytes 884744 | tf_op jit(solution)/shard_map/ppermute | solution.py:309
  45.3 1.8 %shard_map.85 = (f32[4,7,64,128]{3,2,1,0:T(8,128)S(1)}, f32[2,9,64,128]{3,2,1,0:T(8,128)S(1)}, bf16[2,9,64,128]{3,2,1,0:T(8,128)(2,1)S(1)}) custom-call(s32[10,32]{1,0:T(8,128)S(1)} %bitcast_add_fusion.codes, bf16[8,64,256]{2,1,0:T(8,128)(2,1)S(1)} %all-to-all-done.columns, bf16[32,10,128,128]{3,2,1,0:T(8,128)(2,1)S(1)} %bitcast.23, ...), custom_call_target="tpu_custom_call" | custom-call | flops 2000000000 | bytes 3200000 | tf_op jit(solution)/shard_map/pallas_call | solution.py:156
  47.0 5.7 %collective-permute-done.12.arrived = bf16[4,7,64,128]{3,2,1,0:T(8,128)(2,1)S(1)} collective-permute-done((bf16[4,7,64,128]{3,2,1,0:T(8,128)(2,1)S(1)}, bf16[4,7,64,128]{3,2,1,0:T(8,128)(2,1)S(1)}, u32[]{:S(2)}, u32[]{:S(2)}) %collective-permute-start.12) | collective-permute-done | bytes 458784 | tf_op jit(solution)/shard_map/ppermute | solution.py:305
  54.1 2.1 %collective-permute-start.3 = (bf16[2,9,64,128]{3,2,1,0:T(8,128)(2,1)S(1)}, bf16[2,9,64,128]{3,2,1,0:T(8,128)(2,1)S(1)}, u32[]{:S(2)}, u32[]{:S(2)}) collective-permute-start(bf16[2,9,64,128]{3,2,1,0:T(8,128)(2,1)S(1)} %get-tuple-element.27), channel_id=1, source_target_pairs={{0,16},{16,0},{1,17},{17,1},{2,18},{18,2},{3,19},{19,3},{4,20},{20... | collective-permute-start | bytes 884744 | tf_op jit(solution)/shard_map/ppermute | solution.py:309
  56.3 1.8 %shard_map.84 = (f32[4,7,64,128]{3,2,1,0:T(8,128)S(1)}, f32[2,9,64,128]{3,2,1,0:T(8,128)S(1)}, bf16[2,9,64,128]{3,2,1,0:T(8,128)(2,1)S(1)}) custom-call(s32[10,32]{1,0:T(8,128)S(1)} %bitcast_add_fusion.codes, bf16[8,64,256]{2,1,0:T(8,128)(2,1)S(1)} %all-to-all-done.columns, bf16[32,10,128,128]{3,2,1,0:T(8,128)(2,1)S(1)} %bitcast.24, ...), custom_call_target="tpu_custom_call" | custom-call | flops 2000000000 | bytes 3200000 | tf_op jit(solution)/shard_map/pallas_call | solution.py:156
  58.0 4.5 %collective-permute-done.13.arrived = bf16[4,7,64,128]{3,2,1,0:T(8,128)(2,1)S(1)} collective-permute-done((bf16[4,7,64,128]{3,2,1,0:T(8,128)(2,1)S(1)}, bf16[4,7,64,128]{3,2,1,0:T(8,128)(2,1)S(1)}, u32[]{:S(2)}, u32[]{:S(2)}) %collective-permute-start.13) | collective-permute-done | bytes 458784 | tf_op jit(solution)/shard_map/ppermute | solution.py:305
  62.7 2.2 %collective-permute-start.2 = (bf16[2,9,64,128]{3,2,1,0:T(8,128)(2,1)S(1)}, bf16[2,9,64,128]{3,2,1,0:T(8,128)(2,1)S(1)}, u32[]{:S(2)}, u32[]{:S(2)}) collective-permute-start(bf16[2,9,64,128]{3,2,1,0:T(8,128)(2,1)S(1)} %get-tuple-element.25), channel_id=1, source_target_pairs={{0,16},{16,0},{1,17},{17,1},{2,18},{18,2},{3,19},{19,3},{4,20},{20... | collective-permute-start | bytes 884744 | tf_op jit(solution)/shard_map/ppermute | solution.py:309
  67.1 5.9 %collective-permute-done.2.crossed = bf16[2,9,64,128]{3,2,1,0:T(8,128)(2,1)S(1)} collective-permute-done((bf16[2,9,64,128]{3,2,1,0:T(8,128)(2,1)S(1)}, bf16[2,9,64,128]{3,2,1,0:T(8,128)(2,1)S(1)}, u32[]{:S(2)}, u32[]{:S(2)}) %collective-permute-start.2) | collective-permute-done | bytes 294944 | tf_op jit(solution)/shard_map/ppermute | solution.py:309
  73.0 2.5 %collective-permute-done.9.rest_0_ = bf16[2,9,64,128]{3,2,1,0:T(8,128)(2,1)S(1)} collective-permute-done((bf16[2,9,64,128]{3,2,1,0:T(8,128)(2,1)S(1)}, bf16[2,9,64,128]{3,2,1,0:T(8,128)(2,1)S(1)}, u32[]{:S(2)}, u32[]{:S(2)}) %collective-permute-start.9) | collective-permute-done | bytes 294944 | tf_op jit(solution)/shard_map/ppermute | solution.py:305
  77.2 2.2 %collective-permute-start.1 = (bf16[1,9,64,128]{3,2,1,0:T(8,128)(2,1)S(1)}, bf16[1,9,64,128]{3,2,1,0:T(8,128)(2,1)S(1)}, u32[]{:S(2)}, u32[]{:S(2)}) collective-permute-start(bf16[1,9,64,128]{3,2,1,0:T(8,128)(2,1)S(1)} %get-tuple-element.23), channel_id=1, source_target_pairs={{0,16},{16,0},{1,17},{17,1},{2,18},{18,2},{3,19},{19,3},{4,20},{20... | collective-permute-start | bytes 442376 | tf_op jit(solution)/shard_map/ppermute | solution.py:309
  79.4 4.3 %collective-permute-done.10.arrived.near_same = bf16[2,9,64,128]{3,2,1,0:T(8,128)(2,1)S(1)} collective-permute-done((bf16[2,9,64,128]{3,2,1,0:T(8,128)(2,1)S(1)}, bf16[2,9,64,128]{3,2,1,0:T(8,128)(2,1)S(1)}, u32[]{:S(2)}, u32[]{:S(2)}) %collective-permute-start.10) | collective-permute-done | bytes 294944 | tf_op jit(solution)/shard_map/ppermute | solution.py:305
  83.9 2.2 %collective-permute-start.16 = (bf16[7,64,128]{2,1,0:T(8,128)(2,1)S(1)}, bf16[7,64,128]{2,1,0:T(8,128)(2,1)S(1)}, u32[]{:S(2)}, u32[]{:S(2)}) collective-permute-start(bf16[7,64,128]{2,1,0:T(8,128)(2,1)S(1)} %shard_map.99), channel_id=1, source_target_pairs={{0,16},{16,0},{1,17},{17,1},{2,18},{18,2},{3,19},{19,3},{4,20},{20... | collective-permute-start | bytes 344072 | tf_op jit(solution)/shard_map/ppermute | solution.py:309
  86.1 4.9 %collective-permute-done.16.late_cross = bf16[7,64,128]{2,1,0:T(8,128)(2,1)S(1)} collective-permute-done((bf16[7,64,128]{2,1,0:T(8,128)(2,1)S(1)}, bf16[7,64,128]{2,1,0:T(8,128)(2,1)S(1)}, u32[]{:S(2)}, u32[]{:S(2)}) %collective-permute-start.16) | collective-permute-done | bytes 114720 | tf_op jit(solution)/shard_map/ppermute | solution.py:309
  91.8 4.5 %all-to-all-start.1 = ((bf16[8,2,64,128]{3,2,1,0:T(8,128)(2,1)}), bf16[8,2,64,128]{3,2,1,0:T(8,128)(2,1)S(1)}, u32[]{:S(2)}, u32[]{:S(2)}) async-start(bf16[8,2,64,128]{3,2,1,0:T(8,128)(2,1)} %shard_map.100), calls=%async_computation.1 | async-start | bytes 524288 | tf_op jit(solution)/shard_map/all_to_all | solution.py:357
  96.7 5.8 %all-to-all-done.1.neighbors = bf16[8,2,64,128]{3,2,1,0:T(8,128)(2,1)S(1)} async-done(((bf16[8,2,64,128]{3,2,1,0:T(8,128)(2,1)}), bf16[8,2,64,128]{3,2,1,0:T(8,128)(2,1)S(1)}, u32[]{:S(2)}, u32[]{:S(2)}) %all-to-all-start.1) | async-done | bytes 262176 | tf_op jit(solution)/shard_map/all_to_all | solution.py:357
  (53 shorter events, 13.9 us)
Async XLA Ops:
  0.0 96.3 %copy-start = (bf16[512,512]{1,0:T(8,128)(2,1)S(1)}, bf16[512,512]{1,0:T(8,128)(2,1)}, u32[]{:S(2)}) copy-start(bf16[512,512]{1,0:T(8,128)(2,1)} %param.14) | copy-start | bytes 1572868
  0.0 12.2 %all-to-all-start = ((bf16[8,64,256]{2,1,0:T(8,128)(2,1)}), bf16[8,64,256]{2,1,0:T(8,128)(2,1)S(1)}, u32[]{:S(2)}, u32[]{:S(2)}) async-start(bf16[8,64,256]{2,1,0:T(8,128)(2,1)} %bitcast.27), calls=%async_computation | async-start | bytes 524288 | tf_op jit(solution)/shard_map/all_to_all | solution.py:315
  19.2 26.1 %collective-permute-start = (bf16[10,16,64,128]{3,2,1,0:T(8,128)(2,1)S(1)}, bf16[10,16,64,128]{3,2,1,0:T(8,128)(2,1)S(1)}, u32[]{:S(2)}, u32[]{:S(2)}) collective-permute-start(bf16[10,16,64,128]{3,2,1,0:T(8,128)(2,1)S(1)} %shard_map.82), channel_id=1, source_target_pairs={{0,8},{8,0},{1,9},{9,1},{2,10},{10,2},{3,11},{11,3},{4,12},{12,4},... | collective-permute-start | bytes 7864328 | tf_op jit(solution)/shard_map/ppermute | solution.py:309
  21.0 24.2 %slice-start = ((s8[10485760]{0:T(1024)(128)(4,1)}), s8[4194304]{0:T(1024)(128)(4,1)S(1)}, s32[]{:S(2)}) async-start(s8[10485760]{0:T(1024)(128)(4,1)} %bitcast.21), calls=%async_computation.2 | async-start | bytes 8388608
  21.0 24.2 %slice-start.1 = ((s8[10485760]{0:T(1024)(128)(4,1)}), s8[4194304]{0:T(1024)(128)(4,1)S(1)}, s32[]{:S(2)}) async-start(s8[10485760]{0:T(1024)(128)(4,1)} %bitcast.21), calls=%async_computation.3 | async-start | bytes 8388608
  24.6 7.1 %collective-permute-start.4 = (bf16[4,16,64,128]{3,2,1,0:T(8,128)(2,1)S(1)}, bf16[4,16,64,128]{3,2,1,0:T(8,128)(2,1)S(1)}, u32[]{:S(2)}, u32[]{:S(2)}) collective-permute-start(bf16[4,16,64,128]{3,2,1,0:T(8,128)(2,1)S(1)} %get-tuple-element.29), channel_id=1, source_target_pairs={{0,8},{8,0},{1,9},{9,1},{2,10},{10,2},{3,11},{11,3},{4,12},{12,4},... | collective-permute-start | bytes 3145736 | tf_op jit(solution)/shard_map/ppermute | solution.py:309
  26.4 18.8 %slice-start.2 = ((s8[10485760]{0:T(1024)(128)(4,1)}), s8[2097152]{0:T(1024)(128)(4,1)S(1)}, s32[]{:S(2)}) async-start(s8[10485760]{0:T(1024)(128)(4,1)} %bitcast.21), calls=%async_computation.4 | async-start | bytes 4194304
  26.4 2.0 %collective-permute-start.5 = (bf16[2,16,64,128]{3,2,1,0:T(8,128)(2,1)S(1)}, bf16[2,16,64,128]{3,2,1,0:T(8,128)(2,1)S(1)}, u32[]{:S(2)}, u32[]{:S(2)}) collective-permute-start(bf16[2,16,64,128]{3,2,1,0:T(8,128)(2,1)S(1)} %shard_map.89), channel_id=1, source_target_pairs={{0,8},{8,0},{1,9},{9,1},{2,10},{10,2},{3,11},{11,3},{4,12},{12,4},... | collective-permute-start | bytes 1572872 | tf_op jit(solution)/shard_map/ppermute | solution.py:309
  29.7 13.1 %collective-permute-start.6 = (bf16[2,16,64,128]{3,2,1,0:T(8,128)(2,1)S(1)}, bf16[2,16,64,128]{3,2,1,0:T(8,128)(2,1)S(1)}, u32[]{:S(2)}, u32[]{:S(2)}) collective-permute-start(bf16[2,16,64,128]{3,2,1,0:T(8,128)(2,1)S(1)} %shard_map.90), channel_id=1, source_target_pairs={{0,32},{8,232},{32,64},{40,8},{64,96},{72,40},{96,128},{104,72},{1... | collective-permute-start | bytes 1572872 | tf_op jit(solution)/shard_map/ppermute | solution.py:305
  42.9 9.8 %collective-permute-start.12 = (bf16[4,7,64,128]{3,2,1,0:T(8,128)(2,1)S(1)}, bf16[4,7,64,128]{3,2,1,0:T(8,128)(2,1)S(1)}, u32[]{:S(2)}, u32[]{:S(2)}) collective-permute-start(bf16[4,7,64,128]{3,2,1,0:T(8,128)(2,1)S(1)} %get-tuple-element.38), channel_id=1, source_target_pairs={{0,32},{8,232},{32,64},{40,8},{64,96},{72,40},{96,128},{104,72},{1... | collective-permute-start | bytes 1376264 | tf_op jit(solution)/shard_map/ppermute | solution.py:305
  43.0 10.6 %collective-permute-start.7 = (bf16[2,9,64,128]{3,2,1,0:T(8,128)(2,1)S(1)}, bf16[2,9,64,128]{3,2,1,0:T(8,128)(2,1)S(1)}, u32[]{:S(2)}, u32[]{:S(2)}) collective-permute-start(bf16[2,9,64,128]{3,2,1,0:T(8,128)(2,1)S(1)} %get-tuple-element.34), channel_id=1, source_target_pairs={{0,16},{16,0},{1,17},{17,1},{2,18},{18,2},{3,19},{19,3},{4,20},{20... | collective-permute-start | bytes 884744 | tf_op jit(solution)/shard_map/ppermute | solution.py:309
  52.8 9.8 %collective-permute-start.13 = (bf16[4,7,64,128]{3,2,1,0:T(8,128)(2,1)S(1)}, bf16[4,7,64,128]{3,2,1,0:T(8,128)(2,1)S(1)}, u32[]{:S(2)}, u32[]{:S(2)}) collective-permute-start(bf16[4,7,64,128]{3,2,1,0:T(8,128)(2,1)S(1)} %shard_map.96), channel_id=1, source_target_pairs={{0,32},{8,232},{32,64},{40,8},{64,96},{72,40},{96,128},{104,72},{1... | collective-permute-start | bytes 1376264 | tf_op jit(solution)/shard_map/ppermute | solution.py:305
  53.7 12.0 %collective-permute-start.8 = (bf16[2,9,64,128]{3,2,1,0:T(8,128)(2,1)S(1)}, bf16[2,9,64,128]{3,2,1,0:T(8,128)(2,1)S(1)}, u32[]{:S(2)}, u32[]{:S(2)}) collective-permute-start(bf16[2,9,64,128]{3,2,1,0:T(8,128)(2,1)S(1)} %shard_map.92), channel_id=1, source_target_pairs={{0,32},{8,232},{32,64},{40,8},{64,96},{72,40},{96,128},{104,72},{1... | collective-permute-start | bytes 884744 | tf_op jit(solution)/shard_map/ppermute | solution.py:305
  54.1 11.6 %collective-permute-start.3 = (bf16[2,9,64,128]{3,2,1,0:T(8,128)(2,1)S(1)}, bf16[2,9,64,128]{3,2,1,0:T(8,128)(2,1)S(1)}, u32[]{:S(2)}, u32[]{:S(2)}) collective-permute-start(bf16[2,9,64,128]{3,2,1,0:T(8,128)(2,1)S(1)} %get-tuple-element.27), channel_id=1, source_target_pairs={{0,16},{16,0},{1,17},{17,1},{2,18},{18,2},{3,19},{19,3},{4,20},{20... | collective-permute-start | bytes 884744 | tf_op jit(solution)/shard_map/ppermute | solution.py:309
  62.6 13.1 %collective-permute-start.14 = (bf16[4,7,64,128]{3,2,1,0:T(8,128)(2,1)S(1)}, bf16[4,7,64,128]{3,2,1,0:T(8,128)(2,1)S(1)}, u32[]{:S(2)}, u32[]{:S(2)}) collective-permute-start(bf16[4,7,64,128]{3,2,1,0:T(8,128)(2,1)S(1)} %shard_map.97), channel_id=1, source_target_pairs={{0,32},{8,232},{32,64},{40,8},{64,96},{72,40},{96,128},{104,72},{1... | collective-permute-start | bytes 1376264 | tf_op jit(solution)/shard_map/ppermute | solution.py:305
  62.7 10.3 %collective-permute-start.2 = (bf16[2,9,64,128]{3,2,1,0:T(8,128)(2,1)S(1)}, bf16[2,9,64,128]{3,2,1,0:T(8,128)(2,1)S(1)}, u32[]{:S(2)}, u32[]{:S(2)}) collective-permute-start(bf16[2,9,64,128]{3,2,1,0:T(8,128)(2,1)S(1)} %get-tuple-element.25), channel_id=1, source_target_pairs={{0,16},{16,0},{1,17},{17,1},{2,18},{18,2},{3,19},{19,3},{4,20},{20... | collective-permute-start | bytes 884744 | tf_op jit(solution)/shard_map/ppermute | solution.py:309
  65.8 9.8 %collective-permute-start.9 = (bf16[2,9,64,128]{3,2,1,0:T(8,128)(2,1)S(1)}, bf16[2,9,64,128]{3,2,1,0:T(8,128)(2,1)S(1)}, u32[]{:S(2)}, u32[]{:S(2)}) collective-permute-start(bf16[2,9,64,128]{3,2,1,0:T(8,128)(2,1)S(1)} %shard_map.93), channel_id=1, source_target_pairs={{0,32},{8,232},{32,64},{40,8},{64,96},{72,40},{96,128},{104,72},{1... | collective-permute-start | bytes 884744 | tf_op jit(solution)/shard_map/ppermute | solution.py:305
  75.7 8.0 %collective-permute-start.10 = (bf16[2,9,64,128]{3,2,1,0:T(8,128)(2,1)S(1)}, bf16[2,9,64,128]{3,2,1,0:T(8,128)(2,1)S(1)}, u32[]{:S(2)}, u32[]{:S(2)}) collective-permute-start(bf16[2,9,64,128]{3,2,1,0:T(8,128)(2,1)S(1)} %shard_map.94), channel_id=1, source_target_pairs={{0,32},{8,232},{32,64},{40,8},{64,96},{72,40},{96,128},{104,72},{1... | collective-permute-start | bytes 884744 | tf_op jit(solution)/shard_map/ppermute | solution.py:305
  75.8 8.0 %collective-permute-start.15 = (bf16[2,7,64,128]{3,2,1,0:T(8,128)(2,1)S(1)}, bf16[2,7,64,128]{3,2,1,0:T(8,128)(2,1)S(1)}, u32[]{:S(2)}, u32[]{:S(2)}) collective-permute-start(bf16[2,7,64,128]{3,2,1,0:T(8,128)(2,1)S(1)} %shard_map.98), channel_id=1, source_target_pairs={{0,8},{8,0},{1,9},{9,1},{2,10},{10,2},{3,11},{11,3},{4,12},{12,4},... | collective-permute-start | bytes 688136 | tf_op jit(solution)/shard_map/ppermute | solution.py:309
  77.2 8.9 %collective-permute-start.1 = (bf16[1,9,64,128]{3,2,1,0:T(8,128)(2,1)S(1)}, bf16[1,9,64,128]{3,2,1,0:T(8,128)(2,1)S(1)}, u32[]{:S(2)}, u32[]{:S(2)}) collective-permute-start(bf16[1,9,64,128]{3,2,1,0:T(8,128)(2,1)S(1)} %get-tuple-element.23), channel_id=1, source_target_pairs={{0,16},{16,0},{1,17},{17,1},{2,18},{18,2},{3,19},{19,3},{4,20},{20... | collective-permute-start | bytes 442376 | tf_op jit(solution)/shard_map/ppermute | solution.py:309
  83.7 2.4 %collective-permute-start.11 = (bf16[1,9,64,128]{3,2,1,0:T(8,128)(2,1)S(1)}, bf16[1,9,64,128]{3,2,1,0:T(8,128)(2,1)S(1)}, u32[]{:S(2)}, u32[]{:S(2)}) collective-permute-start(bf16[1,9,64,128]{3,2,1,0:T(8,128)(2,1)S(1)} %shard_map.95), channel_id=1, source_target_pairs={{0,8},{8,0},{1,9},{9,1},{2,10},{10,2},{3,11},{11,3},{4,12},{12,4},... | collective-permute-start | bytes 442376 | tf_op jit(solution)/shard_map/ppermute | solution.py:309
  83.8 18.7 %copy-start.2 = (bf16[512,512]{1,0:T(8,128)(2,1)S(1)}, bf16[512,512]{1,0:T(8,128)(2,1)}, u32[]{:S(2)}) copy-start(bf16[512,512]{1,0:T(8,128)(2,1)} %weight.1) | copy-start | bytes 1572868
  83.9 7.1 %collective-permute-start.16 = (bf16[7,64,128]{2,1,0:T(8,128)(2,1)S(1)}, bf16[7,64,128]{2,1,0:T(8,128)(2,1)S(1)}, u32[]{:S(2)}, u32[]{:S(2)}) collective-permute-start(bf16[7,64,128]{2,1,0:T(8,128)(2,1)S(1)} %shard_map.99), channel_id=1, source_target_pairs={{0,16},{16,0},{1,17},{17,1},{2,18},{18,2},{3,19},{19,3},{4,20},{20... | collective-permute-start | bytes 344072 | tf_op jit(solution)/shard_map/ppermute | solution.py:309
  91.8 10.7 %all-to-all-start.1 = ((bf16[8,2,64,128]{3,2,1,0:T(8,128)(2,1)}), bf16[8,2,64,128]{3,2,1,0:T(8,128)(2,1)S(1)}, u32[]{:S(2)}, u32[]{:S(2)}) async-start(bf16[8,2,64,128]{3,2,1,0:T(8,128)(2,1)} %shard_map.100), calls=%async_computation.1 | async-start | bytes 524288 | tf_op jit(solution)/shard_map/all_to_all | solution.py:357
  (3 other events, 30.4 us)
